TPU v7x, 256 devices: a whole 4x4x8 slice. The times are simulated.
256 devices in a mesh: seq: 32 (over z, y), head: 8 (over x, core).
Axes of the slice: x: 4, y: 4, z: 8, core: 2. Of those that a mesh axis runs over, the one named last changes fastest.
Arguments:
- query: bfloat16 [16384, 4096], P('seq', 'head'), may hold values from -9 to 9
- keys: bfloat16 [16384, 1024], P('seq', 'head'), may hold values from -9 to 9
- values: bfloat16 [16384, 1024], P('seq', 'head'), may hold values from -6 to 6
- grad_out: bfloat16 [16384, 4096], P('seq', 'head'), may hold values from -6 to 6
- w_query: bfloat16 [4096, 4096], P(None, 'head'), may hold values from -0.5 to 0.5
- w_key: bfloat16 [4096, 1024], P(None, 'head'), may hold values from -0.5 to 0.5
- w_value: bfloat16 [4096, 1024], P(None, 'head'), may hold values from -0.5 to 0.5
- rand_owner: int32 [256, 3], replicated, may hold values from 0 to 31, all different within a row; in each aligned block of 8 rows (0 to 7, 8 to 15, ...) at most 2 rows name the same one
- rand_block: int32 [256, 3], replicated, may hold values from 0 to 7
Outputs:
- grad_input: bfloat16 [16384, 4096], P(('seq', 'head'))
Inputs may be any that keep to these rules, and one draw needn't show every extreme that they name: `rand_owner`: the 3 entries of a row differ; among the rows of one run of 8 query blocks (aligned blocks of rows) no value appears more than 2 times.
All inputs are finite; a program needn't handle non-finite values.
Results may differ from a plain program's by a relative error of at most 0.014.
Values may be sent and summed in bfloat16 or wider, within the bound.
A program may use at most 128 MiB of HBM per device.

v0:
```python
import jax
import jax.numpy as jnp
from jax import lax
from jax.sharding import PartitionSpec as P

HEAD_DIM = 128
BLOCK = 64
GLOBAL = 2
RANDOM = 3
LIST = 8


def with_halo(array, sides, width):
    for axis, dim in sides:
        size, length = (lax.axis_size(axis), array.shape[dim])
        up = [(i, (i + 1) % size) for i in range(size - 1)]
        down = [(j, i) for i, j in up]
        last = lax.slice_in_dim(array, length - width, length, axis=dim)
        first = lax.slice_in_dim(array, 0, width, axis=dim)
        before = lax.ppermute(last, axis, up)
        after = lax.ppermute(first, axis, down)
        array = jnp.concatenate([before, array, after], axis=dim)
    return array


def slot_places(owners, peers):
    onehot = (owners[:, None] == jnp.arange(peers, dtype=jnp.int32)[None, :]).astype(jnp.int32)
    before = jnp.cumsum(onehot, axis=0) - onehot
    return jnp.sum(before * onehot, axis=1)


def on_device(query, keys, values, grad_out, w_query, w_key, w_value, rand_owner, rand_block):
    tok_rows, q_width = query.shape
    k_width = keys.shape[1]
    row_width = 2 * k_width
    kv_local = k_width // HEAD_DIM
    group_size = q_width // k_width
    seq_count = lax.axis_size("seq")
    own_index = lax.axis_index("seq")
    blocks = tok_rows // BLOCK
    capacity = max(2, 3 * ((blocks * RANDOM + seq_count - 1) // seq_count) // 2)
    slot_count = capacity + GLOBAL
    scale = HEAD_DIM ** (-0.5)
    packed = jnp.concatenate([keys, values], axis=1)
    extended = with_halo(packed, (("seq", 0),), BLOCK)
    local_blocks = packed.reshape(blocks, BLOCK, row_width)
    owners_all = rand_owner.reshape(seq_count, blocks * RANDOM)
    picks_all = rand_block.reshape(seq_count, blocks * RANDOM)
    places_all = jax.vmap(lambda owner_row: slot_places(owner_row, seq_count))(owners_all)
    sources = jnp.broadcast_to(jnp.arange(seq_count, dtype=jnp.int32)[:, None], owners_all.shape)
    targets = jnp.where(owners_all == own_index, sources, seq_count)
    send_index = jnp.zeros((seq_count, slot_count), jnp.int32)
    send_index = send_index.at[:, capacity:].set(
        jnp.broadcast_to(jnp.arange(GLOBAL, dtype=jnp.int32)[None, :], (seq_count, GLOBAL))
    )
    send_index = send_index.at[targets, places_all].set(picks_all, mode="drop")
    outgoing = local_blocks[send_index]
    fetched = lax.all_to_all(outgoing, "seq", split_axis=0, concat_axis=0, tiled=True)
    table = jnp.concatenate(
        [
            extended.reshape(blocks + 2, BLOCK, row_width),
            fetched.reshape(seq_count * slot_count, BLOCK, row_width),
        ],
        axis=0,
    )
    global_first = blocks + 2 + capacity
    my_owner = lax.dynamic_slice_in_dim(owners_all, own_index, 1, 0)[0]
    my_place = lax.dynamic_slice_in_dim(places_all, own_index, 1, 0)[0]
    random_index = (blocks + 2 + my_owner * slot_count + my_place).reshape(blocks, RANDOM)
    local_ids = jnp.arange(blocks, dtype=jnp.int32)
    window_index = jnp.stack([local_ids, local_ids + 1, local_ids + 2], axis=1)
    global_index = jnp.broadcast_to(
        global_first + jnp.arange(GLOBAL, dtype=jnp.int32)[None, :], (blocks, GLOBAL)
    )
    key_lists = jnp.concatenate([window_index, global_index, random_index], axis=1)
    global_ids = own_index * blocks + local_ids
    left_usable = global_ids > 0
    right_usable = global_ids < seq_count * blocks - 1
    always = jnp.ones((blocks,), dtype=bool)
    usable = jnp.concatenate(
        [
            jnp.stack([left_usable, always, right_usable], axis=1),
            jnp.ones((blocks, GLOBAL + RANDOM), dtype=bool),
        ],
        axis=1,
    )
    limit = max(1, 512 // BLOCK)
    per_step = max(
        (factor for factor in range(1, blocks + 1) if blocks % factor == 0 and factor <= limit)
    )
    steps_count = blocks // per_step
    q_steps = query.reshape(steps_count, per_step, BLOCK, kv_local, group_size, HEAD_DIM)
    do_steps = grad_out.reshape(steps_count, per_step, BLOCK, kv_local, group_size, HEAD_DIM)
    list_steps = key_lists.reshape(steps_count, per_step, LIST)
    usable_steps = usable.reshape(steps_count, per_step, LIST)

    def attend(gtable, items):
        q_block, do_block, list_block, usable_block = items
        gathered = table[list_block].reshape(per_step, LIST * BLOCK, 2, kv_local, HEAD_DIM)
        key_rows = gathered[:, :, 0]
        value_rows = gathered[:, :, 1]
        scores = (
            jnp.einsum("pihgd,pjhd->phgij", q_block, key_rows, preferred_element_type=jnp.float32)
            * scale
        )
        mask = jnp.repeat(usable_block, BLOCK, axis=1)[:, None, None, None, :]
        scores = jnp.where(mask, scores, -1e30)
        row_max = jnp.max(scores, axis=-1, keepdims=True)
        powers = jnp.exp(scores - row_max)
        attn_weights = powers / jnp.sum(powers, axis=-1, keepdims=True)
        weights_half = attn_weights.astype(jnp.bfloat16)
        attn_out = jnp.einsum(
            "phgij,pjhd->pihgd", weights_half, value_rows, preferred_element_type=jnp.float32
        )
        delta = jnp.sum(do_block.astype(jnp.float32) * attn_out, axis=-1)
        dprob = jnp.einsum(
            "pihgd,pjhd->phgij", do_block, value_rows, preferred_element_type=jnp.float32
        )
        dscore = attn_weights * (dprob - jnp.transpose(delta, (0, 2, 3, 1))[..., None])
        dscore_half = dscore.astype(jnp.bfloat16)
        grad_query = (
            jnp.einsum(
                "phgij,pjhd->pihgd", dscore_half, key_rows, preferred_element_type=jnp.float32
            )
            * scale
        ).astype(jnp.bfloat16)
        key_part = (
            jnp.einsum(
                "phgij,pihgd->pjhd", dscore_half, q_block, preferred_element_type=jnp.float32
            )
            * scale
        )
        value_part = jnp.einsum(
            "phgij,pihgd->pjhd", weights_half, do_block, preferred_element_type=jnp.float32
        )
        partial_value = jnp.stack([key_part, value_part], axis=2).reshape(
            per_step, LIST, BLOCK, row_width
        )
        return (gtable.at[list_block].add(partial_value), grad_query)

    table_rows = table.shape[0]
    start_table = jnp.zeros((table_rows, BLOCK, row_width), jnp.float32)
    gtable, dq_steps = lax.scan(attend, start_table, (q_steps, do_steps, list_steps, usable_steps))
    grad_query = dq_steps.reshape(tok_rows, q_width)
    local_part = gtable[1 : blocks + 1]
    rims = jnp.concatenate([gtable[0], gtable[blocks + 1]], axis=0)
    rim_back = with_halo(rims.astype(jnp.bfloat16), (("seq", 0),), BLOCK).astype(rims.dtype)
    local_part = local_part.at[0].add(rim_back[:BLOCK])
    local_part = local_part.at[blocks - 1].add(rim_back[3 * BLOCK :])
    region = (
        gtable[blocks + 2 : blocks + 2 + seq_count * slot_count]
        .reshape(seq_count, slot_count, BLOCK, row_width)
        .astype(jnp.bfloat16)
    )
    remote_random = region[:, :capacity]
    run_half = gtable[global_first : global_first + GLOBAL].astype(jnp.bfloat16)
    first_peer = (jnp.arange(seq_count, dtype=jnp.int32) == 0)[:, None, None, None]
    global_slots = jnp.where(first_peer, run_half[None], jnp.zeros_like(run_half)[None])
    returned = jnp.concatenate([remote_random, global_slots], axis=1)
    arrived = lax.all_to_all(returned, "seq", split_axis=0, concat_axis=0, tiled=True)
    local_part = local_part.at[send_index].add(arrived.astype(jnp.float32))
    grad_kv = local_part.astype(jnp.bfloat16).reshape(tok_rows, row_width)
    grad_keys = grad_kv[:, :k_width]
    grad_values = grad_kv[:, k_width:]
    term = jnp.einsum("tc,dc->td", grad_query, w_query, preferred_element_type=jnp.float32)
    term = term + jnp.einsum("tc,dc->td", grad_keys, w_key, preferred_element_type=jnp.float32)
    term = term + jnp.einsum("tc,dc->td", grad_values, w_value, preferred_element_type=jnp.float32)
    return lax.psum_scatter(term.astype(jnp.bfloat16), "head", scatter_dimension=0, tiled=True)


def solution(mesh):
    return jax.shard_map(
        on_device,
        mesh=mesh,
        in_specs=(
            P("seq", "head"),
            P("seq", "head"),
            P("seq", "head"),
            P("seq", "head"),
            P(None, "head"),
            P(None, "head"),
            P(None, "head"),
            P(),
            P(),
        ),
        out_specs=P(("seq", "head"), None),
        check_vma=False,
    )
```

profile of v0, /device:TPU:2, one launch (start us, length us, event | category | flops | bytes accessed | tf_op | source)
XLA Modules:
  0.0 395.4 jit_solution(8389676812942358926)
XLA Ops:
  6.5 0.9 copy.36
  7.4 0.7 broadcast_compare_fusion
  8.7 0.8 fusion.64
  9.7 0.8 copy.39
  10.8 0.7 scatter.12
  11.5 33.3 %scatter_fusion = s32[32,4]{0,1:T(4,128)S(1)} fusion(s32[32,4]{0,1:T(4,128)S(1)} %scatter.12, s32[768]{0:T(1024)S(1)} %reshape.473, s32[768]{0:T(1024)S(1)} %reshape.475), kind=kCustom, calls=%fused_computation.2 | custom fusion | bytes 15360 | tf_op jit(solution)/shard_map/scatter | solution.py:56
  45.1 2.7 gather_fusion
  47.9 11.7 %all-to-all-start = ((bf16[32,4,64,256]{3,2,1,0:T(8,128)(2,1)}), bf16[32,4,64,256]{3,2,1,0:T(8,128)(2,1)}, u32[]{:S(2)}, u32[]{:S(2)}) async-start(bf16[32,4,64,256]{3,2,1,0:T(8,128)(2,1)} %bitcast.178), calls=%async_computation | async-start | bytes 8388608 | tf_op jit(solution)/shard_map/all_to_all | solution.py:58
  59.6 3.6 collective-permute-start
  63.3 1.3 collective-permute-start.1
  65.5 0.9 reshape.448
  66.4 1.4 reshape.456
  68.0 0.9 reshape.446
  68.9 2.3 collective-permute-done
  71.2 3.5 collective-permute-done.1
  74.7 79.2 %all-to-all-done = bf16[32,4,64,256]{3,2,1,0:T(8,128)(2,1)} async-done(((bf16[32,4,64,256]{3,2,1,0:T(8,128)(2,1)}), bf16[32,4,64,256]{3,2,1,0:T(8,128)(2,1)}, u32[]{:S(2)}, u32[]{:S(2)}) %all-to-all-start) | async-done | bytes 4194336 | tf_op jit(solution)/shard_map/all_to_all | solution.py:58
  153.9 4.6 %pad_maximum_fusion = bf16[138,64,256]{2,1,0:T(8,128)(2,1)} fusion(bf16[128,64,256]{2,1,0:T(8,128)(2,1)} %bitcast.4, bf16[10,64,256]{2,1,0:T(8,128)(2,1)S(1)} %bitcast.183), kind=kLoop, calls=%fused_computation.6 | loop fusion | flops 2260992 | bytes 9043968 | tf_op jit(solution)/shard_map/concatenate | solution.py:59
  158.5 4.3 %gather_fusion.1 = bf16[64,64,256]{2,1,0:T(8,128)(2,1)} fusion(bf16[138,64,256]{2,1,0:T(8,128)(2,1)} %pad_maximum_fusion, s32[1024]{0:T(1024)S(1)} %pad_clamp_fusion), kind=kCustom, calls=%fused_computation.1 | custom fusion | bytes 4194560 | tf_op jit(solution)/shard_map/while/body/eval_jaxpr/gather | solution.py:99
  162.8 2.5 reshape.444
  165.4 3.0 fusion.62
  168.4 1.3 copy-done.2
  169.7 0.8 bitcast_reduce_fusion
  170.5 1.9 fusion.4
  172.4 2.5 fusion.15
  174.9 1.6 fusion.32
  176.6 1.7 fusion.1
  178.3 0.8 fusion.5
  179.5 5.2 %copy.52 = f32[8,512,2,1,128]{4,2,1,0,3:T(2,128)} copy(f32[8,512,2,1,128]{4,1,0,3,2:T(8,128)S(1)} %pad_maximum_fusion.1) | data formatting | bytes 8388608 | tf_op jit(solution)/shard_map/while/body/eval_jaxpr/stack | solution.py:136
  184.7 6.5 %reshape.483 = f32[64,64,256]{2,1,0:T(8,128)} reshape(f32[8,512,2,1,128]{4,2,1,0,3:T(2,128)} %copy.52) | data formatting | bytes 8388608 | tf_op jit(solution)/shard_map/while/body/eval_jaxpr/reshape | solution.py:136
  191.2 4.6 %broadcast_in_dim.103 = f32[138,64,256]{2,1,0:T(8,128)} broadcast(f32[]{:T(128)} %constant.154.clone.1), dimensions={} | broadcast | bytes 9043972 | tf_op jit(solution)/shard_map/broadcast_in_dim | solution.py:142
  195.8 13.7 %scatter_fusion.1 = f32[138,64,256]{2,1,0:T(8,128)} fusion(f32[138,64,256]{2,1,0:T(8,128)} %broadcast_in_dim.103, s32[64]{0:T(128)S(1)} %reshape.467, f32[64,64,256]{2,1,0:T(8,128)} %reshape.483), kind=kCustom, calls=%fused_computation.3 | custom fusion | flops 1048576 | bytes 12583168 | tf_op jit(solution)/shard_map/while/body/eval_jaxpr/scatter-add | solution.py:139
  209.4 4.3 %convert.11 = bf16[138,64,256]{2,1,0:T(8,128)(2,1)S(1)} convert(f32[138,64,256]{2,1,0:T(8,128)} %scatter_fusion.1) | non-fusion elementwise | flops 2260992 | bytes 13565952 | tf_op jit(solution)/shard_map/convert.6
  214.3 1.6 copy-done.1
  216.9 2.4 pad_maximum_fusion.2
  219.3 7.2 %all-to-all-start.1 = ((bf16[32,4,64,256]{3,2,1,0:T(8,128)(2,1)}), bf16[32,4,64,256]{3,2,1,0:T(8,128)(2,1)}, u32[]{:S(2)}, u32[]{:S(2)}) async-start(bf16[32,4,64,256]{3,2,1,0:T(8,128)(2,1)} %pad_maximum_fusion.2), calls=%async_computation.1 | async-start | bytes 8388608 | tf_op jit(solution)/shard_map/all_to_all | solution.py:160
  226.6 0.9 slice_bitcast_fusion.1
  227.6 3.7 collective-permute-start.2
  231.3 1.3 collective-permute-start.3
  232.6 2.3 fusion.36
  235.3 5.6 %fusion.39 = f32[512,4096]{1,0:T(8,128)} fusion(bf16[4096,512]{1,0:T(8,128)(2,1)S(1)} %copy-done.3, bf16[64,8,4,128]{3,2,1,0:T(4,128)(2,1)S(1)} %bitcast.180), kind=kOutput, calls=%fused_computation.42 | convolution fusion | flops 2147483648 | bytes 13107200 | tf_op jit(solution)/shard_map/tc,dc->td/dot_general | solution.py:165
  241.0 1.1 slice.137
  242.1 0.9 fusion.54
  243.0 77.9 %all-to-all-done.1 = bf16[32,4,64,256]{3,2,1,0:T(8,128)(2,1)} async-done(((bf16[32,4,64,256]{3,2,1,0:T(8,128)(2,1)}), bf16[32,4,64,256]{3,2,1,0:T(8,128)(2,1)}, u32[]{:S(2)}, u32[]{:S(2)}) %all-to-all-start.1) | async-done | bytes 4194336 | tf_op jit(solution)/shard_map/all_to_all | solution.py:160
  320.9 6.5 %bitcast_convert_fusion = f32[128,64,256]{2,1,0:T(8,128)} fusion(bf16[32,4,64,256]{3,2,1,0:T(8,128)(2,1)} %all-to-all-done.1), kind=kLoop, calls=%fused_computation.9 | loop fusion | flops 2097152 | bytes 12582912 | tf_op jit(solution)/shard_map/convert_element_type | solution.py:161
  327.4 17.0 %scatter_fusion.2 = f32[8,64,256]{2,1,0:T(8,128)S(1)} fusion(f32[8,64,256]{2,1,0:T(8,128)S(1)} %fusion.52, s32[128]{0:T(128)S(1)} %reshape.459, f32[128,64,256]{2,1,0:T(8,128)} %bitcast_convert_fusion), kind=kCustom, calls=%fused_computation.4 | custom fusion | flops 2097152 | bytes 25166336 | tf_op jit(solution)/shard_map/scatter-add | solution.py:161
  344.4 1.3 fusion.50
  345.7 6.8 %add_convert_fusion = bf16[512,4096]{1,0:T(8,128)(2,1)} fusion(f32[512,4096]{1,0:T(8,128)} %fusion.39, f32[512,4096]{1,0:T(8,128)S(1)} %fusion.50, bf16[4096,128]{1,0:T(8,128)(2,1)S(1)} %copy-done.7, bf16[512,256]{1,0:T(8,128)(2,1)S(1)} %bitcast.182), kind=kOutput, calls=%fused_computation.5 | convolution fusion | flops 543162368 | bytes 22151168 | tf_op jit(solution)/shard_map/tc,dc->td/dot_general | solution.py:167
  352.5 36.0 %reduce-scatter.2.cloned.1.call-done = bf16[64,4096]{1,0:T(8,128)(2,1)} async-done(((bf16[512,4096]{1,0:T(8,128)(2,1)}), bf16[64,4096]{1,0:T(8,128)(2,1)}) %reduce-scatter.2.cloned.1.call-update) | async-done | bytes 524304 | tf_op jit(solution)/shard_map/reduce_scatter | solution.py:168
  (73 shorter events, 4.8 us)
Async XLA Ops:
  6.5 337.9 %copy-start = (bf16[4096,128]{1,0:T(8,128)(2,1)S(1)}, bf16[4096,128]{1,0:T(8,128)(2,1)}, u32[]{:S(2)}) copy-start(bf16[4096,128]{1,0:T(8,128)(2,1)} %param.20) | copy-start | bytes 3145732
  11.5 33.5 %copy-start.10 = (bf16[512,128]{1,0:T(8,128)(2,1)S(1)}, bf16[512,128]{1,0:T(8,128)(2,1)}, u32[]{:S(2)}) copy-start(bf16[512,128]{1,0:T(8,128)(2,1)} %param.16) | copy-start | bytes 393220
  11.5 33.6 %copy-start.11 = (bf16[512,128]{1,0:T(8,128)(2,1)S(1)}, bf16[512,128]{1,0:T(8,128)(2,1)}, u32[]{:S(2)}) copy-start(bf16[512,128]{1,0:T(8,128)(2,1)} %param.17) | copy-start | bytes 393220
  47.9 17.6 %copy-start.4 = (bf16[512,512]{1,0:T(8,128)(2,1)S(1)}, bf16[512,512]{1,0:T(8,128)(2,1)}, u32[]{:S(2)}) copy-start(bf16[512,512]{1,0:T(8,128)(2,1)} %param.18) | copy-start | bytes 1572868
  47.9 20.1 %copy-start.8 = (bf16[512,512]{1,0:T(8,128)(2,1)S(1)}, bf16[512,512]{1,0:T(8,128)(2,1)}, u32[]{:S(2)}) copy-start(bf16[512,512]{1,0:T(8,128)(2,1)} %param.15) | copy-start | bytes 1572868
  47.9 106.0 %all-to-all-start = ((bf16[32,4,64,256]{3,2,1,0:T(8,128)(2,1)}), bf16[32,4,64,256]{3,2,1,0:T(8,128)(2,1)}, u32[]{:S(2)}, u32[]{:S(2)}) async-start(bf16[32,4,64,256]{3,2,1,0:T(8,128)(2,1)} %bitcast.178), calls=%async_computation | async-start | bytes 8388608 | tf_op jit(solution)/shard_map/all_to_all | solution.py:58
  59.6 11.6 %collective-permute-start = (bf16[64,256]{1,0:T(8,128)(2,1)S(1)}, bf16[64,256]{1,0:T(8,128)(2,1)S(1)}, u32[]{:S(2)}, u32[]{:S(2)}) collective-permute-start(bf16[64,256]{1,0:T(8,128)(2,1)S(1)} %get-tuple-element.69), channel_id=1, source_target_pairs={{0,8},{8,16},{16,24},{24,32},{32,40},{40,48},{48,56},{56,64},{64,7... | collective-permute-start | bytes 98312 | tf_op jit(solution)/shard_map/ppermute | solution.py:20
  63.3 11.4 %collective-permute-start.1 = (bf16[64,256]{1,0:T(8,128)(2,1)S(1)}, bf16[64,256]{1,0:T(8,128)(2,1)S(1)}, u32[]{:S(2)}, u32[]{:S(2)}) collective-permute-start(bf16[64,256]{1,0:T(8,128)(2,1)S(1)} %get-tuple-element.70), channel_id=1, source_target_pairs={{8,0},{16,8},{24,16},{32,24},{40,32},{48,40},{56,48},{64,56},{72,6... | collective-permute-start | bytes 98312 | tf_op jit(solution)/shard_map/ppermute | solution.py:21
  165.4 4.3 %copy-start.5 = (bf16[8,64,4,128]{3,2,1,0:T(4,128)(2,1)S(1)}, bf16[8,64,4,128]{3,2,1,0:T(4,128)(2,1)}, u32[]{:S(2)}) copy-start(bf16[8,64,4,128]{3,2,1,0:T(4,128)(2,1)} %reshape.446) | copy-start | bytes 1572868
  168.4 1.3 copy-start.2
  169.7 2.8 copy-start.9
  172.4 2.5 copy-start.6
  213.7 2.2 copy-start.1
  215.9 0.8 slice-start
  219.3 101.5 %all-to-all-start.1 = ((bf16[32,4,64,256]{3,2,1,0:T(8,128)(2,1)}), bf16[32,4,64,256]{3,2,1,0:T(8,128)(2,1)}, u32[]{:S(2)}, u32[]{:S(2)}) async-start(bf16[32,4,64,256]{3,2,1,0:T(8,128)(2,1)} %pad_maximum_fusion.2), calls=%async_computation.1 | async-start | bytes 8388608 | tf_op jit(solution)/shard_map/all_to_all | solution.py:160
  226.6 162.0 %reduce-scatter.2.cloned.1.call-start = ((), (), s32[]{:S(2)}) async-start(), calls=%async_computation.3 | async-start | bytes 4718592 | tf_op jit(solution)/shard_map/reduce_scatter | solution.py:168
  226.6 8.7 %copy-start.3 = (bf16[4096,512]{1,0:T(8,128)(2,1)S(1)}, bf16[4096,512]{1,0:T(8,128)(2,1)}, u32[]{:S(2)}) copy-start(bf16[4096,512]{1,0:T(8,128)(2,1)} %param.19) | copy-start | bytes 12582916
  227.6 14.5 %collective-permute-start.2 = (bf16[64,256]{1,0:T(8,128)(2,1)S(1)}, bf16[64,256]{1,0:T(8,128)(2,1)S(1)}, u32[]{:S(2)}, u32[]{:S(2)}) collective-permute-start(bf16[64,256]{1,0:T(8,128)(2,1)S(1)} %get-tuple-element.65), channel_id=1, source_target_pairs={{0,8},{8,16},{16,24},{24,32},{32,40},{40,48},{48,56},{56,64},{64,7... | collective-permute-start | bytes 98312 | tf_op jit(solution)/shard_map/ppermute | solution.py:20
  231.3 10.8 %collective-permute-start.3 = (bf16[64,256]{1,0:T(8,128)(2,1)S(1)}, bf16[64,256]{1,0:T(8,128)(2,1)S(1)}, u32[]{:S(2)}, u32[]{:S(2)}) collective-permute-start(bf16[64,256]{1,0:T(8,128)(2,1)S(1)} %get-tuple-element.66), channel_id=1, source_target_pairs={{8,0},{16,8},{24,16},{32,24},{40,32},{48,40},{56,48},{64,56},{72,6... | collective-permute-start | bytes 98312 | tf_op jit(solution)/shard_map/ppermute | solution.py:21
  344.4 1.3 copy-start.7
Sparse Core Ops, SparseCore 0:
  352.7 35.8 reduce-scatter.1
where the time goes:
time: 400 us; the launch traced here: 395 us
  waiting for transfers between devices  199 us (50%)
  local copies, waits for them, and re-layouts  76.5 us (19%)
  other arithmetic  53.7 us (13%)
  starting transfers between devices  29 us (7%)
  matrix products  23.5 us (6%)
  between operations  13.8 us (3%)
    all_to_all x1, waiting for transfers between devices, on_device(): lax.all_to_all(outgoing, 'seq', split_axis=0, concat_axis=0, tiled=True)  79.2 us
    all_to_all x1, waiting for transfers between devices, on_device(): lax.all_to_all(returned, 'seq', split_axis=0, concat_axis=0, tiled=True)  77.9 us
    reduce_scatter x1, waiting for transfers between devices, on_device(): lax.psum_scatter(term.astype(jnp.bfloat16), 'head', scatter_dimension=0,...  36 us
    scatter x1, local copies, waits for them, and re-layouts, on_device(): send_index = send_index.at[targets, places_all].set(picks_all, mode='drop')  33.3 us
    scatter-add x1, other arithmetic, on_device(): local_part = local_part.at[send_index].add(arrived.astype(jnp.float32))  17 us
    scatter-add x1, other arithmetic, attend(): return (gtable.at[list_block].add(partial_value), grad_query)  13.7 us
    all_to_all x1, starting transfers between devices, on_device(): lax.all_to_all(outgoing, 'seq', split_axis=0, concat_axis=0, tiled=True)  11.7 us
  transfers between devices with their start and end apart: 7, of which 5 were waited for; matrix products, arithmetic and copies ran while one was open for 4% of the time, Pallas kernels for 0%

commit v1 on v0

v1 whole, which is shorter than its diff:
```python
import functools

import jax
import jax.numpy as jnp
from jax import lax
from jax.experimental import pallas as pl
from jax.experimental.pallas import tpu as pltpu
from jax.sharding import PartitionSpec as P

BLOCK = 64
HD = 128
NZ = 8
NY = 4
NX = 4
RUN = 8
ROWS = RUN * BLOCK
GROUP = 4
D = 4096
SLOT0 = NZ * RUN
EXTRA0 = SLOT0 + 3 * 2 * NZ
TABLE = EXTRA0 + 4
REL = (0, 1, 3, 2)
MESH = pl.DeviceIdType.MESH
SCALE = HD ** (-0.5)
VM = pltpu.VMEM


def vmem():
    return pl.BlockSpec(memory_space=pltpu.VMEM)


def smem():
    return pl.BlockSpec(memory_space=pltpu.SMEM)


def seq_place():
    s = lax.axis_index("seq")
    return s, lax.div(s, NY), lax.rem(s, NY)


def rows_of(start, size):
    return pl.ds(pl.multiple_of(start, BLOCK), size)


def prep_kernel(owner_ref, block_ref, picks_ref, list_ref, slot_ref, count_ref):
    s, z, y = seq_place()
    for i in range(4):
        for n in range(32):
            count_ref[i * 32 + n] = 0
        for n in range(16):
            picks_ref[i * 16 + n] = -1
            picks_ref[72 + i * 16 + n] = 0

    for i in range(4):
        row0 = (z * NY + lax.rem(y + REL[i], NY)) * RUN

        def per_row(b, carry):
            for j in range(3):
                owner = owner_ref[row0 + b, j]
                pick = block_ref[row0 + b, j]
                place = count_ref[i * 32 + owner]
                count_ref[i * 32 + owner] = place + 1
                zo = lax.div(owner, NY)
                yo = lax.rem(owner, NY)
                at = zo * 2 + place
                slot = jnp.where(yo == y, i * 16 + at, 64 + j)
                picks_ref[slot] = pick
                picks_ref[72 + slot] = pick
                if i == 0:
                    rel = lax.rem(yo - y + NY, NY)
                    reg = jnp.where(rel == 3, 2, jnp.where(rel == 2, 3, rel))
                    list_ref[b * 8 + 5 + j] = jnp.where(
                        reg == 0, zo * RUN + pick, SLOT0 + (reg - 1) * 16 + at
                    )
                    slot_ref[b * 3 + j] = reg * 16 + at
            if i == 0:
                list_ref[b * 8] = jnp.where(b == 0, EXTRA0, z * RUN + b - 1)
                list_ref[b * 8 + 1] = z * RUN + b
                list_ref[b * 8 + 2] = jnp.where(b == RUN - 1, EXTRA0 + 1, z * RUN + b + 1)
                list_ref[b * 8 + 3] = EXTRA0 + 2
                list_ref[b * 8 + 4] = EXTRA0 + 3
            return carry

        lax.fori_loop(0, RUN, per_row, 0)


def neighbours(z, y):
    return (
        lax.rem(z + 1, NZ) * NY + y,
        lax.rem(z + NZ - 1, NZ) * NY + y,
        z * NY + lax.rem(y + 1, NY),
        z * NY + lax.rem(y + 3, NY),
        z * NY + lax.rem(y + 2, NY),
    )


def greet(peers, axis):
    barrier = pltpu.get_barrier_semaphore()
    for peer in peers:
        pl.semaphore_signal(barrier, inc=1, device_id={axis: peer}, device_id_type=MESH)
    pl.semaphore_wait(barrier, len(peers))


def send(src, dst, ssem, rsem, axis, peer):
    return pltpu.make_async_remote_copy(
        src_ref=src,
        dst_ref=dst,
        send_sem=ssem,
        recv_sem=rsem,
        device_id={axis: peer},
        device_id_type=MESH,
    )


def fetch_kernel(
    picks_ref, k_ref, v_ref, tab, stage, sendbuf, zs, zr, ys, yr, hs, hr, gs, gr
):
    s, z, y = seq_place()
    zu, zd, yp, ym, y2 = neighbours(z, y)
    ypeers = (yp, ym, y2)
    theirs = (1, 0, 2)
    own = (k_ref, v_ref)
    greet((zu, zd, yp, ym, y2), "seq")

    def ring(up, t, kv):
        chunk = lax.rem(z + (NZ - t if up else t), NZ)
        where = tab.at[kv, rows_of(chunk * ROWS, ROWS)]
        i = 0 if up else 1
        return send(
            own[kv] if t == 0 else where, where, zs.at[i, t, kv], zr.at[i, t, kv],
            "seq", zu if up else zd,
        )

    def landed(up, t, kv):
        chunk = lax.rem(z + (NZ - 1 - t if up else 1 + t), NZ)
        where = tab.at[kv, rows_of(chunk * ROWS, ROWS)]
        i = 0 if up else 1
        return send(where, where, zs.at[i, t, kv], zr.at[i, t, kv], "seq", zu if up else zd)

    def slot_copy(p, chunk):
        at = rows_of((SLOT0 + theirs[p] * 16 + chunk * 2) * BLOCK, 2 * BLOCK)
        return send(
            sendbuf.at[p, chunk], tab.at[:, at, :], ys.at[p, chunk], yr.at[theirs[p], chunk],
            "seq", ypeers[p],
        )

    def global_copy(p):
        return send(
            tab.at[:, pl.ds(0, 2 * BLOCK), :],
            tab.at[:, pl.ds((EXTRA0 + 2) * BLOCK, 2 * BLOCK), :],
            gs.at[p], gr, "seq", ypeers[p],
        )

    def halo_copy(p):
        if p == 0:
            chunk = lax.rem(z + NZ - lax.div(y, 3), NZ)
            row = chunk * ROWS + (RUN - 1) * BLOCK
        else:
            chunk = lax.rem(z + lax.div(3 - y, 3), NZ)
            row = chunk * ROWS
        at = pl.ds((EXTRA0 + p) * BLOCK, BLOCK)
        return send(
            tab.at[:, rows_of(row, BLOCK), :], tab.at[:, at, :], hs.at[p], hr.at[p],
            "seq", ypeers[p],
        )

    def spread(chunk):
        for kv in range(2):
            stage[kv] = tab[kv, rows_of(chunk * ROWS, ROWS), :].reshape(RUN, BLOCK, HD)
        for p in range(3):
            for k in range(2):
                pick = picks_ref[72 + (p + 1) * 16 + chunk * 2 + k]
                for kv in range(2):
                    sendbuf[p, chunk, kv, k * BLOCK : (k + 1) * BLOCK, :] = stage[kv, pick]
        for p in range(3):
            slot_copy(p, chunk).start()

        @pl.when(jnp.logical_and(chunk == 0, y == 0))
        def _():
            for p in range(3):
                global_copy(p).start()

    for kv in range(2):
        ring(True, 0, kv).start()
        ring(False, 0, kv).start()
    for kv in range(2):
        tab[kv, rows_of(z * ROWS, ROWS), :] = own[kv][...]
    spread(z)
    for t in range(4):
        for kv in range(2):
            for up in (True, False):
                if t == 3 and kv != (0 if up else 1):
                    continue
                landed(up, t, kv).wait_recv()
                if t < 2 or (t == 2 and kv == (0 if up else 1)):
                    ring(up, t + 1, kv).start()
        if t == 0:
            halo_copy(0).start()
            halo_copy(1).start()
        spread(lax.rem(z + NZ - 1 - t, NZ))
        if t < 3:
            spread(lax.rem(z + 1 + t, NZ))

    for c in range(NZ):
        for p in range(3):
            slot_copy(p, c).wait_recv()
    for p in range(2):
        halo_copy(p).wait_recv()

    @pl.when(y == 0)
    def _():
        for kv in range(2):
            tab[kv, (EXTRA0 + 2) * BLOCK : (EXTRA0 + 4) * BLOCK, :] = tab[kv, 0 : 2 * BLOCK, :]
        for p in range(3):
            global_copy(p).wait_send()

    @pl.when(y != 0)
    def _():
        global_copy(0).wait_recv()

    for t in range(4):
        for kv in range(2):
            for up in (True, False):
                if t == 3 and kv != (0 if up else 1):
                    continue
                ring(up, t, kv).wait_send()
    for c in range(NZ):
        for p in range(3):
            slot_copy(p, c).wait_send()
    for p in range(2):
        halo_copy(p).wait_send()


NT = (((1,), (1,)), ((), ()))
NN = (((1,), (0,)), ((), ()))
TN = (((0,), (0,)), ((), ()))


def dot(a, b, dims):
    return lax.dot_general(a, b, dims, preferred_element_type=jnp.float32)


def attend_kernel(
    list_ref, slot_ref, q_ref, do_ref, tab, dq_ref, part, wloc, halo, glob, kl, vl, wacc, gacc
):
    b = pl.program_id(0)
    s = lax.axis_index("seq")

    @pl.when(b == 0)
    def _():
        wacc[...] = jnp.zeros_like(wacc)
        gacc[...] = jnp.zeros_like(gacc)

    for j in range(8):
        at = rows_of(list_ref[b * 8 + j] * BLOCK, BLOCK)
        kl[j * BLOCK : (j + 1) * BLOCK, :] = tab[0, at, :]
        vl[j * BLOCK : (j + 1) * BLOCK, :] = tab[1, at, :]
    q4 = jnp.concatenate([q_ref[:, g * HD : (g + 1) * HD] for g in range(GROUP)], axis=0)
    d4 = jnp.concatenate([do_ref[:, g * HD : (g + 1) * HD] for g in range(GROUP)], axis=0)
    keys = kl[...]
    vals = vl[...]
    scores = dot(keys, q4, NT) * SCALE
    no_left = jnp.logical_and(s == 0, b == 0)
    no_right = jnp.logical_and(s == NZ * NY - 1, b == RUN - 1)
    scores = jnp.concatenate(
        [
            jnp.where(no_left, -1e30, scores[:BLOCK]),
            scores[BLOCK : 2 * BLOCK],
            jnp.where(no_right, -1e30, scores[2 * BLOCK : 3 * BLOCK]),
            scores[3 * BLOCK :],
        ],
        axis=0,
    )
    row_max = jnp.max(scores, axis=0, keepdims=True)
    powers = jnp.exp(scores - row_max)
    weights = powers * (1.0 / jnp.sum(powers, axis=0, keepdims=True))
    weights_half = weights.astype(jnp.bfloat16)
    dprob = dot(vals, d4, NT)
    delta = jnp.sum(weights_half.astype(jnp.float32) * dprob, axis=0, keepdims=True)
    dscore_half = (weights * (dprob - delta)).astype(jnp.bfloat16)
    dq = (dot(dscore_half, keys, TN) * SCALE).astype(jnp.bfloat16)
    for g in range(GROUP):
        dq_ref[:, g * HD : (g + 1) * HD] = dq[g * BLOCK : (g + 1) * BLOCK]
    parts = (dot(dscore_half, q4, NN) * SCALE, dot(weights_half, d4, NN))
    for kv in range(2):
        grad = parts[kv]
        wacc[kv, rows_of(b * BLOCK, 3 * BLOCK), :] += grad[: 3 * BLOCK]
        gacc[kv] += grad[3 * BLOCK : 5 * BLOCK]
        for j in range(3):
            at = rows_of(slot_ref[b * 3 + j] * BLOCK, BLOCK)
            part[kv, at, :] = grad[(5 + j) * BLOCK : (6 + j) * BLOCK].astype(jnp.bfloat16)

    @pl.when(b == RUN - 1)
    def _():
        for kv in range(2):
            wloc[kv] = wacc[kv, BLOCK : BLOCK + ROWS, :]
            halo[kv, :BLOCK, :] = wacc[kv, :BLOCK, :].astype(jnp.bfloat16)
            halo[kv, BLOCK:, :] = wacc[kv, BLOCK + ROWS :, :].astype(jnp.bfloat16)
            glob[kv] = gacc[kv].astype(jnp.bfloat16)


def return_kernel(
    picks_ref, part, wloc, halo, glob, dk_ref, dv_ref,
    ybuf, hbuf, gbuf, acc, zup, zdown, zs, zr, ys, yr, hs, hr, gs, gr
):
    s, z, y = seq_place()
    zu, zd, yp, ym, y2 = neighbours(z, y)
    ypeers = (yp, ym, y2)
    theirs = (1, 0, 2)
    greet((zu, zd, yp, ym, y2), "seq")

    def slot_copy(p, chunk):
        at = rows_of(((p + 1) * 16 + chunk * 2) * BLOCK, 2 * BLOCK)
        return send(
            part.at[:, at, :], ybuf.at[theirs[p], chunk], ys.at[p, chunk],
            yr.at[theirs[p], chunk], "seq", ypeers[p],
        )

    def halo_copy(p):
        half = pl.ds(BLOCK if p == 0 else 0, BLOCK)
        return send(
            halo.at[:, half, :], hbuf.at[theirs[p]], hs.at[p], hr.at[theirs[p]],
            "seq", ypeers[p],
        )

    def global_copy(slot):
        return send(glob, gbuf.at[slot], gs, gr.at[slot], "seq", z * NY)

    order = (4, 3, -3, 2, -2, 1, -1, 0)

    halo_copy(0).start()
    halo_copy(1).start()
    for n in range(1, NY):
        @pl.when(y == n)
        def _():
            global_copy(n - 1).start()
    for off in order:
        chunk = lax.rem(z + off + NZ, NZ)
        for p in range(3):
            slot_copy(p, chunk).start()

    for p in range(2):
        halo_copy(p).wait_recv()

    @pl.when(y == 0)
    def _():
        for n in range(3):
            global_copy(n).wait_recv()

    low_chunk = lax.rem(z + NZ - lax.div(y, 3), NZ)
    high_chunk = lax.rem(z + lax.div(3 - y, 3), NZ)

    def collect(chunk):
        for p in range(3):
            slot_copy(p, chunk).wait_recv()
        picks = [
            [picks_ref[i * 16 + chunk * 2 + k] for k in range(2)] for i in range(4)
        ]

        def one(b, carry):
            for kv in range(2):
                total = jnp.zeros((BLOCK, HD), jnp.float32)
                for i in range(4):
                    for k in range(2):
                        if i == 0:
                            at = rows_of((chunk * 2 + k) * BLOCK, BLOCK)
                            piece = part[kv, at, :]
                        else:
                            piece = ybuf[i - 1, chunk, kv, k * BLOCK : (k + 1) * BLOCK, :]
                        total = total + jnp.where(
                            picks[i][k] == b, piece.astype(jnp.float32), 0.0
                        )
                acc[kv, rows_of(b * BLOCK, BLOCK), :] = total
            return carry

        lax.fori_loop(0, RUN, one, 0)
        last = pl.ds((RUN - 1) * BLOCK, BLOCK)
        first = pl.ds(0, BLOCK)

        @pl.when(chunk == low_chunk)
        def _():
            for kv in range(2):
                acc[kv, last, :] += hbuf[0, kv].astype(jnp.float32)

        @pl.when(chunk == high_chunk)
        def _():
            for kv in range(2):
                acc[kv, first, :] += hbuf[1, kv].astype(jnp.float32)

        @pl.when(jnp.logical_and(chunk == 0, y == 0))
        def _():
            for kv in range(2):
                total = glob[kv].astype(jnp.float32)
                for n in range(3):
                    total = total + gbuf[n, kv].astype(jnp.float32)
                acc[kv, 0 : 2 * BLOCK, :] += total

    bufs = (zup, zdown)
    zpeer = (zu, zd)

    def ring(i, t, kv):
        return send(
            bufs[i].at[0, t, kv], bufs[i].at[1, t, kv], zs.at[i, t, kv], zr.at[i, t, kv],
            "seq", zpeer[i],
        )

    def push(i, t, kv):
        total = acc[kv]
        if t >= 1 and (t >= 2 or kv == i):
            ring(i, t - 1, kv).wait_recv()
            total = total + bufs[i][1, t - 1, kv].astype(jnp.float32)
        bufs[i][0, t, kv] = total.astype(jnp.bfloat16)
        ring(i, t, kv).start()

    collect(lax.rem(z + 4, NZ))
    push(0, 0, 0)
    push(1, 0, 1)
    for t in range(1, 4):
        collect(lax.rem(z + 4 - t, NZ))
        push(0, t, 0)
        push(0, t, 1)
        collect(lax.rem(z + 4 + t, NZ))
        push(1, t, 1)
        push(1, t, 0)
    collect(z)
    outs = (dk_ref, dv_ref)
    for kv in range(2):
        total = acc[kv] + wloc[kv]
        for i in range(2):
            ring(i, 3, kv).wait_recv()
            total = total + bufs[i][1, 3, kv].astype(jnp.float32)
        outs[kv][...] = total.astype(jnp.bfloat16)

    for i in range(2):
        for t in range(4):
            for kv in range(2):
                if t == 0 and kv != i:
                    continue
                ring(i, t, kv).wait_send()
    for c in range(NZ):
        for p in range(3):
            slot_copy(p, c).wait_send()
    for p in range(2):
        halo_copy(p).wait_send()

    @pl.when(y != 0)
    def _():
        global_copy(0).wait_send()


QUARTER = D // 4


def project_kernel(
    dq, dk, dv, wq, wk, wv, out, term, pair, xout, xin, ps, pr, xs, xr
):
    h = lax.axis_index("head")
    x = lax.div(h, 2)
    c = lax.rem(h, 2)
    partner = x * 2 + 1 - c
    peers = (lax.rem(x + 1, NX) * 2 + c, lax.rem(x + NX - 1, NX) * 2 + c)
    greet((partner,) + peers, "head")

    def cols(quarter):
        return pl.ds(quarter * QUARTER, QUARTER)

    def pair_copy(d, quarter):
        return send(
            term.at[d, rows_of((1 - c) * BLOCK, BLOCK), cols(quarter)],
            pair.at[d, :, cols(quarter)], ps.at[d, quarter], pr.at[d, quarter],
            "head", partner,
        )

    def ring(i, t, quarter):
        return send(
            xout.at[i, t, :, cols(quarter)], xin.at[i, t, :, cols(quarter)],
            xs.at[i, t, quarter], xr.at[i, t, quarter], "head", peers[i],
        )

    def compute(d):
        at = rows_of(lax.rem(x + d, NX) * 2 * BLOCK, 2 * BLOCK)
        a_q = dq[at, :]
        a_k = dk[at, :]
        a_v = dv[at, :]
        width = 512
        for quarter in range(4):
            def tile(n, carry):
                w = pl.ds(pl.multiple_of(quarter * QUARTER + n * width, width), width)
                total = dot(a_q, wq[w, :], NT) + dot(a_k, wk[w, :], NT) + dot(a_v, wv[w, :], NT)
                term[d, :, w] = total.astype(jnp.bfloat16)
                return carry

            lax.fori_loop(0, QUARTER // width, tile, 0)
            pair_copy(d, quarter).start()

    def both(d, quarter):
        pair_copy(d, quarter).wait_recv()
        mine = term[d, rows_of(c * BLOCK, BLOCK), cols(quarter)].astype(jnp.float32)
        return mine + pair[d, :, cols(quarter)].astype(jnp.float32)

    def arrived(i, t, quarter):
        ring(i, t, quarter).wait_recv()
        return xin[i, t, :, cols(quarter)].astype(jnp.float32)

    def push(i, t, quarter, total):
        xout[i, t, :, cols(quarter)] = total.astype(jnp.bfloat16)
        ring(i, t, quarter).start()

    compute(2)
    compute(1)
    for n in range(2):
        push(0, 0, n, both(2, n))
        push(1, 0, 2 + n, both(2, 2 + n))
    compute(3)
    for n in range(2):
        push(0, 1, 2 + n, both(1, 2 + n))
        push(1, 1, n, both(3, n))
    compute(0)
    for n in range(2):
        push(0, 1, n, both(1, n) + arrived(0, 0, n))
        push(1, 1, 2 + n, both(3, 2 + n) + arrived(1, 0, 2 + n))
    for quarter in (2, 3, 0, 1):
        total = both(0, quarter) + arrived(0, 1, quarter) + arrived(1, 1, quarter)
        out[:, cols(quarter)] = total.astype(jnp.bfloat16)
    for d in range(4):
        for quarter in range(4):
            pair_copy(d, quarter).wait_send()
    for i in range(2):
        for quarter in range(4):
            if quarter // 2 == i:
                ring(i, 0, quarter).wait_send()
            ring(i, 1, quarter).wait_send()


def sds(shape, dtype=jnp.bfloat16):
    return jax.ShapeDtypeStruct(shape, dtype)


DMA = pltpu.SemaphoreType.DMA


def prep(rand_owner, rand_block):
    return pl.pallas_call(
        prep_kernel,
        out_shape=(sds((144,), jnp.int32), sds((64,), jnp.int32), sds((24,), jnp.int32)),
        in_specs=[smem()] * 2,
        out_specs=(smem(),) * 3,
        scratch_shapes=[pltpu.SMEM((128,), jnp.int32)],
        name="prep",
    )(rand_owner, rand_block)


def fetch(picks, keys, values):
    return pl.pallas_call(
        fetch_kernel,
        out_shape=sds((2, TABLE * BLOCK, HD)),
        in_specs=[smem(), vmem(), vmem()],
        out_specs=vmem(),
        scratch_shapes=[
            VM((2, RUN, BLOCK, HD), jnp.bfloat16),
            VM((3, NZ, 2, 2 * BLOCK, HD), jnp.bfloat16),
            DMA((2, 4, 2)),
            DMA((2, 4, 2)),
            DMA((3, NZ)),
            DMA((3, NZ)),
            DMA((2,)),
            DMA((2,)),
            DMA((3,)),
            DMA,
        ],
        compiler_params=pltpu.CompilerParams(collective_id=0, has_side_effects=True),
        name="fetch",
    )(picks, keys, values)


def attend(lists, slots, query, grad_out, table):
    whole = lambda shape: pl.BlockSpec(shape, lambda b, *_: (0,) * len(shape))
    step = pl.BlockSpec((BLOCK, GROUP * HD), lambda b, *_: (b, 0))
    outs = (
        sds((ROWS, GROUP * HD)),
        sds((2, 64 * BLOCK, HD)),
        sds((2, ROWS, HD), jnp.float32),
        sds((2, 2 * BLOCK, HD)),
        sds((2, 2 * BLOCK, HD)),
    )
    return pl.pallas_call(
        attend_kernel,
        out_shape=outs,
        grid_spec=pltpu.PrefetchScalarGridSpec(
            num_scalar_prefetch=2,
            grid=(RUN,),
            in_specs=[step, step, whole((2, TABLE * BLOCK, HD))],
            out_specs=(step,) + tuple(whole(o.shape) for o in outs[1:]),
            scratch_shapes=[
                VM((ROWS, HD), jnp.bfloat16),
                VM((ROWS, HD), jnp.bfloat16),
                VM((2, ROWS + 2 * BLOCK, HD), jnp.float32),
                VM((2, 2 * BLOCK, HD), jnp.float32),
            ],
        ),
        name="attend",
    )(lists, slots, query, grad_out, table)


def give_back(picks, part, wloc, halo, glob):
    return pl.pallas_call(
        return_kernel,
        out_shape=(sds((ROWS, HD)), sds((ROWS, HD))),
        in_specs=[smem()] + [vmem()] * 4,
        out_specs=(vmem(), vmem()),
        scratch_shapes=[
            VM((3, NZ, 2, 2 * BLOCK, HD), jnp.bfloat16),
            VM((2, 2, BLOCK, HD), jnp.bfloat16),
            VM((3, 2, 2 * BLOCK, HD), jnp.bfloat16),
            VM((2, ROWS, HD), jnp.float32),
            VM((2, 4, 2, ROWS, HD), jnp.bfloat16),
            VM((2, 4, 2, ROWS, HD), jnp.bfloat16),
            DMA((2, 4, 2)),
            DMA((2, 4, 2)),
            DMA((3, NZ)),
            DMA((3, NZ)),
            DMA((2,)),
            DMA((2,)),
            DMA,
            DMA((3,)),
        ],
        compiler_params=pltpu.CompilerParams(collective_id=1, has_side_effects=True),
        name="give_back",
    )(picks, part, wloc, halo, glob)


def project(dq, dk, dv, wq, wk, wv):
    return pl.pallas_call(
        project_kernel,
        out_shape=sds((BLOCK, D)),
        in_specs=[vmem()] * 6,
        out_specs=vmem(),
        scratch_shapes=[
            VM((4, 2 * BLOCK, D), jnp.bfloat16),
            VM((4, BLOCK, D), jnp.bfloat16),
            VM((2, 2, BLOCK, D), jnp.bfloat16),
            VM((2, 2, BLOCK, D), jnp.bfloat16),
            DMA((4, 4)),
            DMA((4, 4)),
            DMA((2, 2, 4)),
            DMA((2, 2, 4)),
        ],
        compiler_params=pltpu.CompilerParams(collective_id=2, has_side_effects=True),
        name="project",
    )(dq, dk, dv, wq, wk, wv)


def on_device(query, keys, values, grad_out, w_query, w_key, w_value, rand_owner, rand_block):
    picks, lists, slots = prep(rand_owner, rand_block)
    table = fetch(picks, keys, values)
    dq, part, wloc, halo, glob = attend(lists, slots, query, grad_out, table)
    dk, dv = give_back(picks, part, wloc, halo, glob)
    return project(dq, dk, dv, w_query, w_key, w_value)


def solution(mesh):
    return jax.shard_map(
        on_device,
        mesh=mesh,
        in_specs=(
            P("seq", "head"),
            P("seq", "head"),
            P("seq", "head"),
            P("seq", "head"),
            P(None, "head"),
            P(None, "head"),
            P(None, "head"),
            P(),
            P(),
        ),
        out_specs=P(("seq", "head"), None),
        check_vma=False,
    )
```

time: 400 us -> 137 us (0.34)
  waiting for transfers between devices: 199 us -> 0 us
  Pallas kernels: 0 us -> 131 us
  local copies, waits for them, and re-layouts: 76.5 us -> 4.82 us
  other arithmetic: 53.7 us -> 0 us
  starting transfers between devices: 29 us -> 0 us
  matrix products: 23.5 us -> 0 us
  between operations: 13.8 us -> 0.04 us
    all_to_all x2 -> x0, waiting for transfers between devices: 157 us -> none  [the longest x1 79.2 us: on_device(): lax.all_to_all(outgoing, 'seq', split_axis=0, concat_axis=0, tiled=True)]
    pallas_call x0 -> x5, Pallas kernels: none -> 131 us  [the longest x1 40.6 us: give_back(): pl.pallas_call(return_kernel, out_shape=(sds((ROWS, HD)), sds((ROWS, HD))...]
    reduce_scatter x1 -> x0, waiting for transfers between devices: 36 us -> none  [on_device(): lax.psum_scatter(term.astype(jnp.bfloat16), 'head', scatter_dimension=0,...]
    scatter x2 -> x0, local copies, waits for them, and re-layouts: 34 us -> none  [the longest x1 33.3 us: on_device(): send_index = send_index.at[targets, places_all].set(picks_all, mode='drop')]
    scatter-add x4 -> x0, other arithmetic: 31.5 us -> none  [the longest x1 17 us: on_device(): local_part = local_part.at[send_index].add(arrived.astype(jnp.float32))]
    dot_general x9 -> x0, matrix products: 23.5 us -> none  [the longest x1 6.8 us: on_device(): jnp.einsum('tc,dc->td', grad_values, w_value, preferred_element_type=jnp....]
    all_to_all x2 -> x0, starting transfers between devices: 19 us -> none  [the longest x1 11.7 us: on_device(): lax.all_to_all(outgoing, 'seq', split_axis=0, concat_axis=0, tiled=True)]
    ppermute x4 -> x0, starting transfers between devices: 9.95 us -> none  [the longest x2 7.36 us: with_halo(): before = lax.ppermute(last, axis, up)]
  transfers between devices with their start and end apart: 7 -> 0, of which waited for: 5 -> 0; matrix products, arithmetic and copies ran while one was open for 4% -> 0% of each run, Pallas kernels for 0% -> 0%
where the time goes in v1:
time: 137 us; the launch traced here: 135 us
  Pallas kernels  131 us (96%)
  local copies, waits for them, and re-layouts  4.82 us (4%)
    pallas_call x1, Pallas kernels, give_back(): pl.pallas_call(return_kernel, out_shape=(sds((ROWS, HD)), sds((ROWS, HD))...  40.6 us
    pallas_call x1, Pallas kernels, fetch(): pl.pallas_call(fetch_kernel, out_shape=sds((2, TABLE * BLOCK, HD)), in_sp...  40.3 us
    pallas_call x1, Pallas kernels, project(): pl.pallas_call(project_kernel, out_shape=sds((BLOCK, D)), in_specs=[vmem(...  30.8 us
    pallas_call x1, Pallas kernels, attend(): pl.pallas_call(attend_kernel, out_shape=outs, grid_spec=pltpu.PrefetchSca...  12.1 us
    pallas_call x1, Pallas kernels, prep(): pl.pallas_call(prep_kernel, out_shape=(sds((144,), jnp.int32), sds((64,),...  6.7 us
    unnamed x3, local copies, waits for them, and re-layouts  4.82 us

profile of v1, /device:TPU:2, one launch (start us, length us, event | category | flops | bytes accessed | tf_op | source)
XLA Modules:
  0.0 135.4 jit_solution(9240934962949681951)
XLA Ops:
  0.0 1.5 %copy.10.owner_ref = s32[256,3]{1,0:T(8,128)} copy(s32[256,3]{0,1:T(4,128)} %param.16) | data formatting | bytes 6144 | tf_op args[7]
  1.5 1.5 %copy.11.block_ref = s32[256,3]{1,0:T(8,128)} copy(s32[256,3]{0,1:T(4,128)} %param.17) | data formatting | bytes 6144 | tf_op args[8]
  3.0 6.7 %prep.1 = (s32[144]{0:T(256)}, s32[64]{0:T(128)}, s32[24]{0:T(128)}) custom-call(s32[256,3]{1,0:T(8,128)} %copy.10.owner_ref, s32[256,3]{1,0:T(8,128)} %copy.11.block_ref), custom_call_target="tpu_custom_call" | custom-call | tf_op jit(solution)/shard_map/prep/pallas_call | solution.py:543
  9.7 40.3 %fetch.1.tab = bf16[2,7424,128]{2,1,0:T(8,128)(2,1)} custom-call(s32[144]{0:T(256)} %get-tuple-element.17.picks_ref, bf16[512,128]{1,0:T(8,128)(2,1)} %k_ref.1, bf16[512,128]{1,0:T(8,128)(2,1)} %v_ref.1), custom_call_target="tpu_custom_call" | custom-call | tf_op jit(solution)/shard_map/fetch/pallas_call | solution.py:554
  50.0 12.1 %attend.1 = (bf16[512,512]{1,0:T(8,128)(2,1)}, bf16[2,4096,128]{2,1,0:T(8,128)(2,1)}, f32[2,512,128]{2,1,0:T(8,128)}, bf16[2,128,128]{2,1,0:T(8,128)(2,1)}, bf16[2,128,128]{2,1,0:T(8,128)(2,1)}) custom-call(s32[64]{0:T(128)} %get-tuple-element.15.list_ref, s32[24]{0:T(128)} %get-tuple-element.16.slot_ref, bf16[512,512]{1,0:T(8,128)(2,1)} %q_ref.1, ...), custom_call_target="tpu_custom_call" | custom-call | tf_op jit(solution)/shard_map/attend/pallas_call | solution.py:586
  62.1 40.6 %give_back.1 = (bf16[512,128]{1,0:T(8,128)(2,1)}, bf16[512,128]{1,0:T(8,128)(2,1)}) custom-call(s32[144]{0:T(256)} %get-tuple-element.17.picks_ref, bf16[2,4096,128]{2,1,0:T(8,128)(2,1)} %get-tuple-element.19.part, f32[2,512,128]{2,1,0:T(8,128)} %get-tuple-element.20.wloc, bf16[2,128,128]{2,1,0:T(8,128)(2,1)} %get-tuple-element.21.halo, ...), custom_call_target="tpu_custom_call" | custom-call | tf_op jit(solution)/shard_map/give_back/pallas_call | solution.py:606
  102.7 30.8 %project.1 = bf16[64,4096]{1,0:T(8,128)(2,1)} custom-call(bf16[512,512]{1,0:T(8,128)(2,1)} %get-tuple-element.18.dq, bf16[512,128]{1,0:T(8,128)(2,1)} %get-tuple-element.23.dk, bf16[512,128]{1,0:T(8,128)(2,1)} %get-tuple-element.24.dv, bf16[4096,512]{1,0:T(8,128)(2,1)} %wq.1, bf16[4096,128]{1,0:T(8,128)(2,1)} %wk.1, bf16[4096,128]{1,0:T(8,128)(2,1)} %wv.1), custom_call_target="tpu_custom_call" | custom-call | tf_op jit(solution)/shard_map/project/pallas_call | solution.py:633
  133.6 1.9 %copy.13 = bf16[64,4096]{1,0:T(8,128)(2,1)} copy(bf16[64,4096]{1,0:T(8,128)(2,1)} %project.1) | data formatting | bytes 1048576

commit v2 on v1

v2 whole, which is shorter than its diff:
```python
import functools

import jax
import jax.numpy as jnp
from jax import lax
from jax.experimental import pallas as pl
from jax.experimental.pallas import tpu as pltpu
from jax.sharding import PartitionSpec as P

BLOCK = 64
HD = 128
NZ = 8
NY = 4
NX = 4
RUN = 8
ROWS = RUN * BLOCK
GROUP = 4
D = 4096
FROM_UP = NZ * RUN
FROM_DOWN = FROM_UP + 3 * NZ
FROM_FAR = FROM_DOWN + 3 * NZ
EXTRA = FROM_FAR + 2 * NZ
TABLE = EXTRA + 4
OUT_UP = 2 * NZ
OUT_DOWN = OUT_UP + 3 * NZ
OUT = OUT_DOWN + 3 * NZ
MESH = pl.DeviceIdType.MESH
SCALE = HD ** (-0.5)
VM = pltpu.VMEM
DMA = pltpu.SemaphoreType.DMA
NT = (((1,), (1,)), ((), ()))
NN = (((1,), (0,)), ((), ()))
TN = (((0,), (0,)), ((), ()))


def vmem():
    return pl.BlockSpec(memory_space=pltpu.VMEM)


def smem():
    return pl.BlockSpec(memory_space=pltpu.SMEM)


def sds(shape, dtype=jnp.bfloat16):
    return jax.ShapeDtypeStruct(shape, dtype)


def dot(a, b, dims):
    return lax.dot_general(a, b, dims, preferred_element_type=jnp.float32)


def seq_place():
    s = lax.axis_index("seq")
    return s, lax.div(s, NY), lax.rem(s, NY)


def rows_of(start, size):
    return pl.ds(pl.multiple_of(start, BLOCK), size)


def neighbours(z, y):
    return (
        lax.rem(z + 1, NZ) * NY + y,
        lax.rem(z + NZ - 1, NZ) * NY + y,
        z * NY + lax.rem(y + 1, NY),
        z * NY + lax.rem(y + 3, NY),
        z * NY + lax.rem(y + 2, NY),
    )


def greet(peers):
    barrier = pltpu.get_barrier_semaphore()
    for axis, peer in peers:
        pl.semaphore_signal(barrier, inc=1, device_id={axis: peer}, device_id_type=MESH)
    pl.semaphore_wait(barrier, len(peers))


def send(src, dst, ssem, rsem, axis, peer):
    return pltpu.make_async_remote_copy(
        src_ref=src,
        dst_ref=dst,
        send_sem=ssem,
        recv_sem=rsem,
        device_id={axis: peer},
        device_id_type=MESH,
    )


def group_prefix(value, lane):
    for shift in (1, 2, 4):
        value = value + jnp.where(lane >= shift, pltpu.roll(value, shift, 1), 0)
    return value


def index_tables(owner_ref, block_ref, z, y):
    low = z < NZ // 2
    owners = jnp.where(low, owner_ref[:, :128], owner_ref[:, 128:])
    picks = jnp.where(low, block_ref[:, :128], block_ref[:, 128:])
    shape = (NZ * NY, 128)
    index = lax.broadcasted_iota(jnp.int32, shape, 0)
    lane = lax.broadcasted_iota(jnp.int32, shape, 1) & 7
    hits = [jnp.broadcast_to(owners[j : j + 1], shape) == index for j in range(3)]
    named = jnp.zeros(shape, jnp.int32)
    chosen = jnp.zeros(shape, jnp.int32)
    for j in range(3):
        named = named + jnp.where(hits[j], 1, 0)
        chosen = chosen + jnp.where(hits[j], jnp.broadcast_to(picks[j : j + 1], shape), 0)
    place = group_prefix(named, lane) - named
    tables = []
    for k in range(2):
        mine = jnp.where((named == 1) & (place == k), chosen + 1, 0)
        tables.append(group_prefix(mine, lane) - 1)
    rows = []
    slots = []
    for j in range(3):
        owner = owners[j : j + 1]
        at = jnp.sum(jnp.where(hits[j], place, 0), axis=0, keepdims=True)
        zo = owner >> 2
        rel = ((owner & 3) - y + NY) & 3
        rows.append(
            jnp.where(
                rel == 0,
                zo * RUN + picks[j : j + 1],
                jnp.where(
                    rel == 2,
                    FROM_FAR + zo * 2 + at,
                    jnp.where(rel == 1, FROM_UP, FROM_DOWN) + zo * 3 + at,
                ),
            )
        )
        slots.append(
            jnp.where(
                rel == 0,
                zo * 2 + at,
                jnp.where(
                    rel == 2,
                    jnp.where(at == 0, OUT_UP, OUT_DOWN) + zo * 3 + 2,
                    jnp.where(rel == 1, OUT_UP, OUT_DOWN) + zo * 3 + at,
                ),
            )
        )
    return tables, rows, slots


def fetch_kernel(
    owner_ref, block_ref, k_ref, v_ref, tab, picks_ref, lists_ref,
    safe_vmem, safe, stage, sendbuf, ts, zs, zr, ys, yr, fs, fr, hs, hr, gs, gr
):
    s, z, y = seq_place()
    zu, zd, yp, ym, y2 = neighbours(z, y)
    ypeers = (yp, ym, y2)
    own = (k_ref, v_ref)
    greet([("seq", n) for n in (zu, zd, yp, ym, y2)])

    def ring(up, t, kv):
        chunk = lax.rem(z + (NZ - t if up else t), NZ)
        where = tab.at[kv, rows_of(chunk * ROWS, ROWS)]
        i = 0 if up else 1
        return send(
            own[kv] if t == 0 else where, where, zs.at[i, t, kv], zr.at[i, t, kv],
            "seq", zu if up else zd,
        )

    def landed(up, t, kv):
        chunk = lax.rem(z + (NZ - 1 - t if up else 1 + t), NZ)
        where = tab.at[kv, rows_of(chunk * ROWS, ROWS)]
        i = 0 if up else 1
        return send(where, where, zs.at[i, t, kv], zr.at[i, t, kv], "seq", zu if up else zd)

    def slot_copy(p, chunk):
        first = (FROM_DOWN, FROM_UP)[p]
        at = rows_of((first + chunk * 3) * BLOCK, 3 * BLOCK)
        return send(
            sendbuf.at[p, chunk], tab.at[:, at, :], ys.at[p, chunk], yr.at[p, chunk],
            "seq", ypeers[p],
        )

    def relay(p, chunk):
        first = (FROM_DOWN, FROM_UP)[p]
        src = rows_of((first + chunk * 3 + 2) * BLOCK, BLOCK)
        at = rows_of((FROM_FAR + chunk * 2 + p) * BLOCK, BLOCK)
        return send(
            tab.at[:, src, :], tab.at[:, at, :], fs.at[p, chunk], fr.at[p, chunk],
            "seq", ypeers[p],
        )

    def global_copy(p):
        return send(
            tab.at[:, pl.ds(0, 2 * BLOCK), :],
            tab.at[:, pl.ds((EXTRA + 2) * BLOCK, 2 * BLOCK), :],
            gs.at[p], gr, "seq", ypeers[p],
        )

    def halo_copy(p):
        if p == 0:
            row = lax.rem(z + NZ - lax.div(y, 3), NZ) * ROWS + (RUN - 1) * BLOCK
        else:
            row = lax.rem(z + lax.div(3 - y, 3), NZ) * ROWS
        at = pl.ds((EXTRA + p) * BLOCK, BLOCK)
        return send(
            tab.at[:, rows_of(row, BLOCK), :], tab.at[:, at, :], hs.at[p], hr.at[p],
            "seq", ypeers[p],
        )

    plane = lax.rem(z, NZ // 2) * (NY * RUN) + RUN - 1

    def spread(chunk):
        for kv in range(2):
            stage[kv] = tab[kv, rows_of(chunk * ROWS, ROWS), :].reshape(RUN, BLOCK, HD)
        for p in range(2):
            wants = [(1 if p == 0 else 3, 0), (1 if p == 0 else 3, 1), (2, p)]
            for n, (rel, k) in enumerate(wants):
                lane = plane + lax.rem(y + rel, NY) * RUN
                pick = safe[k * NZ * NY + chunk * NY + y, lane]
                for kv in range(2):
                    sendbuf[p, chunk, kv, n * BLOCK : (n + 1) * BLOCK, :] = stage[kv, pick]
        for p in range(2):
            slot_copy(p, chunk).start()

        @pl.when(jnp.logical_and(chunk == 0, y == 0))
        def _():
            for p in range(3):
                global_copy(p).start()

    def pass_on(chunk):
        for p in range(2):
            slot_copy(p, chunk).wait_recv()
        for p in range(2):
            relay(p, chunk).start()

    for kv in range(2):
        ring(True, 0, kv).start()
        ring(False, 0, kv).start()
    tables, rows, slots = index_tables(owner_ref, block_ref, z, y)
    for k in range(2):
        part = slice(k * NZ * NY, (k + 1) * NZ * NY)
        picks_ref[part, :] = tables[k]
        safe_vmem[part, :] = jnp.maximum(tables[k], 0)
    to_scalar = pltpu.make_async_copy(safe_vmem, safe, ts)
    to_scalar.start()
    for j in range(3):
        lists_ref[j : j + 1, :] = rows[j]
        lists_ref[3 + j : 4 + j, :] = slots[j]
    for kv in range(2):
        tab[kv, rows_of(z * ROWS, ROWS), :] = own[kv][...]
    to_scalar.wait()
    spread(z)
    before = [z]
    for t in range(4):
        for kv in range(2):
            for up in (True, False):
                if t == 3 and kv != (0 if up else 1):
                    continue
                landed(up, t, kv).wait_recv()
                if t < 2 or (t == 2 and kv == (0 if up else 1)):
                    ring(up, t + 1, kv).start()
        for chunk in before:
            pass_on(chunk)
        if t == 0:
            halo_copy(0).start()
            halo_copy(1).start()
        before = [lax.rem(z + NZ - 1 - t, NZ)]
        if t < 3:
            before.append(lax.rem(z + 1 + t, NZ))
        for chunk in before:
            spread(chunk)
    for chunk in before:
        pass_on(chunk)

    for p in range(2):
        for c in range(NZ):
            relay(p, c).wait_recv()
        halo_copy(p).wait_recv()

    @pl.when(y == 0)
    def _():
        for kv in range(2):
            tab[kv, (EXTRA + 2) * BLOCK : (EXTRA + 4) * BLOCK, :] = tab[kv, 0 : 2 * BLOCK, :]
        for p in range(3):
            global_copy(p).wait_send()

    @pl.when(y != 0)
    def _():
        global_copy(0).wait_recv()

    for t in range(4):
        for kv in range(2):
            for up in (True, False):
                if t == 3 and kv != (0 if up else 1):
                    continue
                ring(up, t, kv).wait_send()
    for p in range(2):
        for c in range(NZ):
            slot_copy(p, c).wait_send()
            relay(p, c).wait_send()
        halo_copy(p).wait_send()


PER = 2


def attend_kernel(
    lists, q_ref, do_ref, tab, dq_ref, part, wloc, halo, glob, kl, vl, wacc, gacc
):
    step = pl.program_id(0)
    s, z, y = seq_place()
    lane0 = (lax.rem(z, NZ // 2) * NY + y) * RUN

    @pl.when(step == 0)
    def _():
        wacc[...] = jnp.zeros_like(wacc)
        gacc[...] = jnp.zeros_like(gacc)

    grads = []
    for n in range(PER):
        b = step * PER + n
        index = [
            jnp.where(b == 0, EXTRA, z * RUN + b - 1),
            z * RUN + b,
            jnp.where(b == RUN - 1, EXTRA + 1, z * RUN + b + 1),
            EXTRA + 2,
            EXTRA + 3,
        ] + [lists[j, lane0 + b] for j in range(3)]
        for j in range(8):
            at = rows_of(index[j] * BLOCK, BLOCK)
            kl[n, j * BLOCK : (j + 1) * BLOCK, :] = tab[0, at, :]
            vl[n, j * BLOCK : (j + 1) * BLOCK, :] = tab[1, at, :]
    for n in range(PER):
        b = step * PER + n
        mine = slice(n * BLOCK, (n + 1) * BLOCK)
        q4 = jnp.concatenate([q_ref[mine, g * HD : (g + 1) * HD] for g in range(GROUP)], axis=0)
        d4 = jnp.concatenate([do_ref[mine, g * HD : (g + 1) * HD] for g in range(GROUP)], axis=0)
        keys = kl[n]
        vals = vl[n]
        scores = dot(keys, q4, NT)
        no_left = jnp.logical_and(s == 0, b == 0)
        no_right = jnp.logical_and(s == NZ * NY - 1, b == RUN - 1)
        scores = jnp.concatenate(
            [
                jnp.where(no_left, -1e30, scores[:BLOCK]),
                scores[BLOCK : 2 * BLOCK],
                jnp.where(no_right, -1e30, scores[2 * BLOCK : 3 * BLOCK]),
                scores[3 * BLOCK :],
            ],
            axis=0,
        )
        row_max = jnp.max(scores, axis=0, keepdims=True)
        powers = jnp.exp((scores - row_max) * SCALE)
        weights = powers * (1.0 / jnp.sum(powers, axis=0, keepdims=True))
        weights_half = weights.astype(jnp.bfloat16)
        dprob = dot(vals, d4, NT)
        delta = jnp.sum(weights_half.astype(jnp.float32) * dprob, axis=0, keepdims=True)
        dscore_half = (weights * (dprob - delta)).astype(jnp.bfloat16)
        dq = (dot(dscore_half, keys, TN) * SCALE).astype(jnp.bfloat16)
        for g in range(GROUP):
            dq_ref[mine, g * HD : (g + 1) * HD] = dq[g * BLOCK : (g + 1) * BLOCK]
        grads.append((dot(dscore_half, q4, NN) * SCALE, dot(weights_half, d4, NN)))
    for n in range(PER):
        b = step * PER + n
        for kv in range(2):
            grad = grads[n][kv]
            wacc[kv, rows_of(b * BLOCK, 3 * BLOCK), :] += grad[: 3 * BLOCK]
            gacc[kv] += grad[3 * BLOCK : 5 * BLOCK]
            for j in range(3):
                at = rows_of(lists[3 + j, lane0 + b] * BLOCK, BLOCK)
                part[kv, at, :] = grad[(5 + j) * BLOCK : (6 + j) * BLOCK].astype(jnp.bfloat16)

    @pl.when(step == RUN // PER - 1)
    def _():
        for kv in range(2):
            wloc[kv] = wacc[kv, BLOCK : BLOCK + ROWS, :]
            halo[kv, :BLOCK, :] = wacc[kv, :BLOCK, :].astype(jnp.bfloat16)
            halo[kv, BLOCK:, :] = wacc[kv, BLOCK + ROWS :, :].astype(jnp.bfloat16)
            glob[kv] = gacc[kv].astype(jnp.bfloat16)


QUARTER = D // 4
TILE = 512


def finish_kernel(
    picks_ref, part, wloc, halo, glob, dq, wq_hbm, wk_hbm, wv_hbm, out,
    wq, wkv, dkv, ybuf, fbuf, hbuf, gbuf, acc, zup, zdown,
    total_ref, term, pair, xout, xin,
    ws, zs, zr, ys, yr, fs, fr, hs, hr, gs, gr, ps, pr, xs, xr
):
    s, z, y = seq_place()
    zu, zd, yp, ym, y2 = neighbours(z, y)
    ypeers = (yp, ym)
    h = lax.axis_index("head")
    x = lax.div(h, 2)
    c = lax.rem(h, 2)
    partner = x * 2 + 1 - c
    xpeers = (lax.rem(x + 1, NX) * 2 + c, lax.rem(x + NX - 1, NX) * 2 + c)
    loads = (
        pltpu.make_async_copy(wq_hbm, wq, ws.at[0]),
        pltpu.make_async_copy(wk_hbm, wkv.at[:, pl.ds(0, HD)], ws.at[1]),
        pltpu.make_async_copy(wv_hbm, wkv.at[:, pl.ds(HD, HD)], ws.at[2]),
    )
    for load in loads:
        load.start()
    greet(
        [("seq", n) for n in (zu, zd, yp, ym, y2)]
        + [("head", n) for n in (partner,) + xpeers]
    )

    def slot_copy(p, chunk):
        first = (OUT_UP, OUT_DOWN)[p]
        at = rows_of((first + chunk * 3) * BLOCK, 3 * BLOCK)
        return send(
            part.at[:, at, :], ybuf.at[p, chunk], ys.at[p, chunk], yr.at[p, chunk],
            "seq", ypeers[p],
        )

    def relay(p, chunk):
        return send(
            ybuf.at[p, chunk, :, pl.ds(2 * BLOCK, BLOCK), :], fbuf.at[p, chunk],
            fs.at[p, chunk], fr.at[p, chunk], "seq", ypeers[p],
        )

    def halo_copy(p):
        half = pl.ds(BLOCK if p == 0 else 0, BLOCK)
        return send(halo.at[:, half, :], hbuf.at[p], hs.at[p], hr.at[p], "seq", ypeers[p])

    def global_copy(slot):
        return send(glob, gbuf.at[slot], gs, gr.at[slot], "seq", z * NY)

    chunks = [lax.rem(z + off + NZ, NZ) for off in (4, 3, -3, 2, -2, 1, -1, 0)]
    low_chunk = lax.rem(z + NZ - lax.div(y, 3), NZ)
    high_chunk = lax.rem(z + lax.div(3 - y, 3), NZ)
    plane = lax.rem(z, NZ // 2) * (NY * RUN) + RUN - 1

    def offer(n):
        for p in range(2):
            slot_copy(p, chunks[n]).start()

    def pass_on(n):
        for p in range(2):
            slot_copy(p, chunks[n]).wait_recv()
        for p in range(2):
            relay(p, chunks[n]).start()

    def collect(n):
        chunk = chunks[n]
        for p in range(2):
            relay(p, chunk).wait_recv()
        pieces = []
        for k in range(2):
            pieces.append((0, k, lambda kv, k=k: part[kv, rows_of((chunk * 2 + k) * BLOCK, BLOCK), :]))
            pieces.append((3, k, lambda kv, k=k: ybuf[0, chunk, kv, k * BLOCK : (k + 1) * BLOCK, :]))
            pieces.append((1, k, lambda kv, k=k: ybuf[1, chunk, kv, k * BLOCK : (k + 1) * BLOCK, :]))
            pieces.append((2, k, lambda kv, k=k: fbuf[k, chunk, kv]))
        picks = [
            picks_ref[k * NZ * NY + chunk * NY + y, plane + lax.rem(y + rel, NY) * RUN]
            for rel, k, _ in pieces
        ]
        for kv in range(2):
            data = [get(kv).astype(jnp.float32) for _, _, get in pieces]

            def one(b, carry):
                total = jnp.where(picks[0] == b, data[0], 0.0)
                for i in range(1, 8):
                    total = total + jnp.where(picks[i] == b, data[i], 0.0)
                acc[kv, rows_of(b * BLOCK, BLOCK), :] = total
                return carry

            lax.fori_loop(0, RUN, one, 0)
        last = pl.ds((RUN - 1) * BLOCK, BLOCK)
        first = pl.ds(0, BLOCK)

        @pl.when(chunk == low_chunk)
        def _():
            for kv in range(2):
                acc[kv, last, :] += hbuf[1, kv].astype(jnp.float32)

        @pl.when(chunk == high_chunk)
        def _():
            for kv in range(2):
                acc[kv, first, :] += hbuf[0, kv].astype(jnp.float32)

        @pl.when(jnp.logical_and(chunk == 0, y == 0))
        def _():
            for kv in range(2):
                total = glob[kv].astype(jnp.float32)
                for m in range(3):
                    total = total + gbuf[m, kv].astype(jnp.float32)
                acc[kv, 0 : 2 * BLOCK, :] += total

    bufs = (zup, zdown)
    zpeer = (zu, zd)

    def zring(i, t, kv):
        return send(
            bufs[i].at[0, t, kv], bufs[i].at[1, t, kv], zs.at[i, t, kv], zr.at[i, t, kv],
            "seq", zpeer[i],
        )

    def zpush(i, t, kv):
        total = acc[kv]
        if t >= 1 and (t >= 2 or kv == i):
            zring(i, t - 1, kv).wait_recv()
            total = total + bufs[i][1, t - 1, kv].astype(jnp.float32)
        bufs[i][0, t, kv] = total.astype(jnp.bfloat16)
        zring(i, t, kv).start()

    def token_rows(d):
        return rows_of(lax.rem(x + d, NX) * 2 * BLOCK, 2 * BLOCK)

    def query_part(d):
        a = dq[token_rows(d), :]

        def tile(n, carry):
            w = pl.ds(pl.multiple_of(n * TILE, TILE), TILE)
            total_ref[d, :, w] = dot(a, wq[w, :], NT)
            return carry

        lax.fori_loop(0, D // TILE, tile, 0)

    halo_copy(0).start()
    halo_copy(1).start()
    offer(0)
    for n in range(1, NY):
        @pl.when(y == n)
        def _():
            global_copy(n - 1).start()
    offer(1)
    for load in loads:
        load.wait()
    query_part(2)
    pass_on(0)
    offer(2)
    for p in range(2):
        halo_copy(p).wait_recv()

    @pl.when(y == 0)
    def _():
        for m in range(3):
            global_copy(m).wait_recv()

    pass_on(1)
    offer(3)
    collect(0)
    zpush(0, 0, 0)
    zpush(1, 0, 1)
    pass_on(2)
    offer(4)
    for t in range(1, 4):
        n = 2 * t - 1
        collect(n)
        zpush(0, t, 0)
        zpush(0, t, 1)
        pass_on(n + 2) if n + 2 < NZ else None
        offer(n + 4) if n + 4 < NZ else None
        collect(n + 1)
        zpush(1, t, 1)
        zpush(1, t, 0)
        pass_on(n + 3) if n + 3 < NZ else None
        offer(n + 5) if n + 5 < NZ else None
        query_part((1, 3, 0)[t - 1])
    collect(7)
    for kv in range(2):
        total = acc[kv] + wloc[kv]
        for i in range(2):
            zring(i, 3, kv).wait_recv()
            total = total + bufs[i][1, 3, kv].astype(jnp.float32)
        dkv[:, kv * HD : (kv + 1) * HD] = total.astype(jnp.bfloat16)

    def cols(quarter):
        return pl.ds(quarter * QUARTER, QUARTER)

    def pair_copy(d, quarter):
        return send(
            term.at[d, rows_of((1 - c) * BLOCK, BLOCK), cols(quarter)],
            pair.at[d, :, cols(quarter)], ps.at[d, quarter], pr.at[d, quarter],
            "head", partner,
        )

    def xring(i, t, quarter):
        return send(
            xout.at[i, t, :, cols(quarter)], xin.at[i, t, :, cols(quarter)],
            xs.at[i, t, quarter], xr.at[i, t, quarter], "head", xpeers[i],
        )

    def compute(d):
        a = dkv[token_rows(d), :]
        for quarter in range(4):
            def tile(n, carry):
                w = pl.ds(pl.multiple_of(quarter * QUARTER + n * TILE, TILE), TILE)
                total = total_ref[d, :, w] + dot(a, wkv[w, :], NT)
                term[d, :, w] = total.astype(jnp.bfloat16)
                return carry

            lax.fori_loop(0, QUARTER // TILE, tile, 0)
            pair_copy(d, quarter).start()

    def both(d, quarter):
        pair_copy(d, quarter).wait_recv()
        mine = term[d, rows_of(c * BLOCK, BLOCK), cols(quarter)].astype(jnp.float32)
        return mine + pair[d, :, cols(quarter)].astype(jnp.float32)

    def arrived(i, t, quarter):
        xring(i, t, quarter).wait_recv()
        return xin[i, t, :, cols(quarter)].astype(jnp.float32)

    def xpush(i, t, quarter, total):
        xout[i, t, :, cols(quarter)] = total.astype(jnp.bfloat16)
        xring(i, t, quarter).start()

    compute(2)
    compute(1)
    for n in range(2):
        xpush(0, 0, n, both(2, n))
        xpush(1, 0, 2 + n, both(2, 2 + n))
    compute(3)
    for n in range(2):
        xpush(0, 1, 2 + n, both(1, 2 + n))
        xpush(1, 1, n, both(3, n))
    compute(0)
    for n in range(2):
        xpush(0, 1, n, both(1, n) + arrived(0, 0, n))
        xpush(1, 1, 2 + n, both(3, 2 + n) + arrived(1, 0, 2 + n))
    for quarter in (2, 3, 0, 1):
        total = both(0, quarter) + arrived(0, 1, quarter) + arrived(1, 1, quarter)
        out[:, cols(quarter)] = total.astype(jnp.bfloat16)

    for i in range(2):
        for t in range(4):
            for kv in range(2):
                if t == 0 and kv != i:
                    continue
                zring(i, t, kv).wait_send()
    for p in range(2):
        for n in range(NZ):
            slot_copy(p, n).wait_send()
            relay(p, n).wait_send()
        halo_copy(p).wait_send()

    @pl.when(y != 0)
    def _():
        global_copy(0).wait_send()

    for d in range(4):
        for quarter in range(4):
            pair_copy(d, quarter).wait_send()
    for i in range(2):
        for quarter in range(4):
            if quarter // 2 == i:
                xring(i, 0, quarter).wait_send()
            xring(i, 1, quarter).wait_send()


def fetch(owners, blocks, keys, values):
    return pl.pallas_call(
        fetch_kernel,
        out_shape=(
            sds((2, TABLE * BLOCK, HD)),
            sds((2 * NZ * NY, 128), jnp.int32),
            sds((8, 128), jnp.int32),
        ),
        in_specs=[vmem()] * 4,
        out_specs=(vmem(),) * 3,
        scratch_shapes=[
            VM((2 * NZ * NY, 128), jnp.int32),
            pltpu.SMEM((2 * NZ * NY, 128), jnp.int32),
            VM((2, RUN, BLOCK, HD), jnp.bfloat16),
            VM((2, NZ, 2, 3 * BLOCK, HD), jnp.bfloat16),
            DMA,
            DMA((2, 4, 2)),
            DMA((2, 4, 2)),
            DMA((2, NZ)),
            DMA((2, NZ)),
            DMA((2, NZ)),
            DMA((2, NZ)),
            DMA((2,)),
            DMA((2,)),
            DMA((3,)),
            DMA,
        ],
        compiler_params=pltpu.CompilerParams(collective_id=0, has_side_effects=True),
        name="fetch",
    )(owners, blocks, keys, values)


def attend(lists, query, grad_out, table):
    whole = lambda shape: pl.BlockSpec(shape, lambda b, *_: (0,) * len(shape))
    step = pl.BlockSpec((PER * BLOCK, GROUP * HD), lambda b, *_: (b, 0))
    outs = (
        sds((ROWS, GROUP * HD)),
        sds((2, OUT * BLOCK, HD)),
        sds((2, ROWS, HD), jnp.float32),
        sds((2, 2 * BLOCK, HD)),
        sds((2, 2 * BLOCK, HD)),
    )
    return pl.pallas_call(
        attend_kernel,
        out_shape=outs,
        grid_spec=pltpu.PrefetchScalarGridSpec(
            num_scalar_prefetch=1,
            grid=(RUN // PER,),
            in_specs=[step, step, whole((2, TABLE * BLOCK, HD))],
            out_specs=(step,) + tuple(whole(o.shape) for o in outs[1:]),
            scratch_shapes=[
                VM((PER, ROWS, HD), jnp.bfloat16),
                VM((PER, ROWS, HD), jnp.bfloat16),
                VM((2, ROWS + 2 * BLOCK, HD), jnp.float32),
                VM((2, 2 * BLOCK, HD), jnp.float32),
            ],
        ),
        name="attend",
    )(lists, query, grad_out, table)


def finish(picks, part, wloc, halo, glob, dq, wq, wk, wv):
    anywhere = pl.BlockSpec(memory_space=pl.ANY)
    return pl.pallas_call(
        finish_kernel,
        out_shape=sds((BLOCK, D)),
        in_specs=[smem()] + [vmem()] * 5 + [anywhere] * 3,
        out_specs=vmem(),
        scratch_shapes=[
            VM((D, GROUP * HD), jnp.bfloat16),
            VM((D, 2 * HD), jnp.bfloat16),
            VM((ROWS, 2 * HD), jnp.bfloat16),
            VM((2, NZ, 2, 3 * BLOCK, HD), jnp.bfloat16),
            VM((2, NZ, 2, BLOCK, HD), jnp.bfloat16),
            VM((2, 2, BLOCK, HD), jnp.bfloat16),
            VM((3, 2, 2 * BLOCK, HD), jnp.bfloat16),
            VM((2, ROWS, HD), jnp.float32),
            VM((2, 4, 2, ROWS, HD), jnp.bfloat16),
            VM((2, 4, 2, ROWS, HD), jnp.bfloat16),
            VM((4, 2 * BLOCK, D), jnp.float32),
            VM((4, 2 * BLOCK, D), jnp.bfloat16),
            VM((4, BLOCK, D), jnp.bfloat16),
            VM((2, 2, BLOCK, D), jnp.bfloat16),
            VM((2, 2, BLOCK, D), jnp.bfloat16),
            DMA((3,)),
            DMA((2, 4, 2)),
            DMA((2, 4, 2)),
            DMA((2, NZ)),
            DMA((2, NZ)),
            DMA((2, NZ)),
            DMA((2, NZ)),
            DMA((2,)),
            DMA((2,)),
            DMA,
            DMA((3,)),
            DMA((4, 4)),
            DMA((4, 4)),
            DMA((2, 2, 4)),
            DMA((2, 2, 4)),
        ],
        compiler_params=pltpu.CompilerParams(collective_id=1, has_side_effects=True),
        name="finish",
    )(picks, part, wloc, halo, glob, dq, wq, wk, wv)


def on_device(query, keys, values, grad_out, w_query, w_key, w_value, rand_owner, rand_block):
    table, picks, lists = fetch(rand_owner.T, rand_block.T, keys, values)
    dq, part, wloc, halo, glob = attend(lists, query, grad_out, table)
    return finish(picks, part, wloc, halo, glob, dq, w_query, w_key, w_value)


def solution(mesh):
    return jax.shard_map(
        on_device,
        mesh=mesh,
        in_specs=(
            P("seq", "head"),
            P("seq", "head"),
            P("seq", "head"),
            P("seq", "head"),
            P(None, "head"),
            P(None, "head"),
            P(None, "head"),
            P(),
            P(),
        ),
        out_specs=P(("seq", "head"), None),
        check_vma=False,
    )
```

time: 137 us -> 127 us (0.927); the launches traced: 135 us -> 127 us
  Pallas kernels: 131 us -> 125 us
  local copies, waits for them, and re-layouts: 4.82 us -> 1.87 us
    pallas_call x4 -> x2, Pallas kernels: 118 us -> 114 us  [the longest x1 66.9 us: finish(): pl.pallas_call(finish_kernel, out_shape=sds((BLOCK, D)), in_specs=[smem()...]
    unnamed x3 -> x1, local copies, waits for them, and re-layouts: 4.82 us -> 1.87 us
where the time goes in v2:
time: 127 us
  Pallas kernels  125 us (98%)
  local copies, waits for them, and re-layouts  1.87 us (1%)
    pallas_call x1, Pallas kernels, finish(): pl.pallas_call(finish_kernel, out_shape=sds((BLOCK, D)), in_specs=[smem()...  66.9 us
    pallas_call x1, Pallas kernels, fetch(): pl.pallas_call(fetch_kernel, out_shape=(sds((2, TABLE * BLOCK, HD)), sds(...  46.8 us
    pallas_call x1, Pallas kernels, attend(): pl.pallas_call(attend_kernel, out_shape=outs, grid_spec=pltpu.PrefetchSca...  11.6 us

profile of v2, /device:TPU:2, one launch (start us, length us, event | category | flops | bytes accessed | tf_op | source)
XLA Modules:
  0.0 127.2 jit_solution(12604340739444320736)
XLA Ops:
  0.0 46.8 %fetch.1 = (bf16[2,8448,128]{2,1,0:T(8,128)(2,1)}, s32[64,128]{1,0:T(8,128)}, s32[8,128]{1,0:T(8,128)}) custom-call(s32[3,256]{1,0:T(4,128)} %bitcast.2, s32[3,256]{1,0:T(4,128)} %bitcast.3, bf16[512,128]{1,0:T(8,128)(2,1)} %k_ref.1, bf16[512,128]{1,0:T(8,128)(2,1)} %v_ref.1), custom_call_target="tpu_custom_call" | custom-call | tf_op jit(solution)/shard_map/fetch/pallas_call | solution.py:653
  46.8 11.6 %attend.1 = (bf16[512,512]{1,0:T(8,128)(2,1)}, bf16[2,4096,128]{2,1,0:T(8,128)(2,1)}, f32[2,512,128]{2,1,0:T(8,128)}, bf16[2,128,128]{2,1,0:T(8,128)(2,1)}, bf16[2,128,128]{2,1,0:T(8,128)(2,1)}) custom-call(s32[8,128]{1,0:T(8,128)} %get-tuple-element.14.lists, bf16[512,512]{1,0:T(8,128)(2,1)} %q_ref.1, bf16[512,512]{1,0:T(8,128)(2,1)} %do_ref.1, ...), custom_call_target="tpu_custom_call" | custom-call | tf_op jit(solution)/shard_map/attend/pallas_call | solution.py:694
  58.4 66.9 %finish.1 = bf16[64,4096]{1,0:T(8,128)(2,1)} custom-call(s32[64,128]{1,0:T(8,128)} %get-tuple-element.13.picks_ref, bf16[2,4096,128]{2,1,0:T(8,128)(2,1)} %get-tuple-element.16.part, f32[2,512,128]{2,1,0:T(8,128)} %get-tuple-element.17.wloc, bf16[2,128,128]{2,1,0:T(8,128)(2,1)} %get-tuple-element.18.halo, bf16[2,128,128]{2,1,0:T(8,128)(2,1)} %get-tuple-element.19.glob, ...), custom_call_target="tpu_custom_call" | custom-call | tf_op jit(solution)/shard_map/finish/pallas_call | solution.py:715
  125.3 1.9 %copy.11 = bf16[64,4096]{1,0:T(8,128)(2,1)} copy(bf16[64,4096]{1,0:T(8,128)(2,1)} %finish.1) | data formatting | bytes 1048576

commit v3 on v0

v3 whole, which is shorter than its diff:
```python
import functools

import jax
import jax.numpy as jnp
from jax import lax
from jax.experimental import pallas as pl
from jax.experimental.pallas import tpu as pltpu
from jax.sharding import PartitionSpec as P

BLOCK = 64
HD = 128
NZ = 8
NY = 4
NX = 4
RUN = 8
ROWS = RUN * BLOCK
GROUP = 4
D = 4096
FROM_UP = NZ * RUN
FROM_DOWN = FROM_UP + 2 * NZ
FROM_FAR = FROM_DOWN + 2 * NZ
EXTRA = FROM_FAR + 2 * NZ
TABLE = EXTRA + 4
OWNERS = NZ * NY
RAW = 2 * OWNERS
ENTRY = 4 * OWNERS
LISTS = 6 * OWNERS
QUARTER = D // 4
TILE = 512
PER = 2
MESH = pl.DeviceIdType.MESH
SCALE = HD ** (-0.5)
VM = pltpu.VMEM
DMA = pltpu.SemaphoreType.DMA
NT = (((1,), (1,)), ((), ()))
NN = (((1,), (0,)), ((), ()))
TN = (((0,), (0,)), ((), ()))


def vmem():
    return pl.BlockSpec(memory_space=pltpu.VMEM)


def sds(shape, dtype=jnp.bfloat16):
    return jax.ShapeDtypeStruct(shape, dtype)


def dot(a, b, dims):
    return lax.dot_general(a, b, dims, preferred_element_type=jnp.float32)


def seq_place():
    s = lax.axis_index("seq")
    return s, lax.div(s, NY), lax.rem(s, NY)


def rows_of(start, size):
    return pl.ds(pl.multiple_of(start, BLOCK), size)


def neighbours(z, y):
    return (
        lax.rem(z + 1, NZ) * NY + y,
        lax.rem(z + NZ - 1, NZ) * NY + y,
        z * NY + lax.rem(y + 1, NY),
        z * NY + lax.rem(y + 3, NY),
        z * NY + lax.rem(y + 2, NY),
    )


def greet(peers):
    barrier = pltpu.get_barrier_semaphore()
    for axis, peer in peers:
        pl.semaphore_signal(barrier, inc=1, device_id={axis: peer}, device_id_type=MESH)
    pl.semaphore_wait(barrier, len(peers))


def send(src, dst, ssem, rsem, axis, peer):
    return pltpu.make_async_remote_copy(
        src_ref=src,
        dst_ref=dst,
        send_sem=ssem,
        recv_sem=rsem,
        device_id={axis: peer},
        device_id_type=MESH,
    )


def group_prefix(value, lane):
    for shift in (1, 2, 4):
        value = value + jnp.where(lane >= shift, pltpu.roll(value, shift, 1), 0)
    return value


def index_tables(owner_ref, block_ref, out, z, y):
    low = z < NZ // 2
    owners = jnp.where(low, owner_ref[:, :128], owner_ref[:, 128:])
    picks = jnp.where(low, block_ref[:, :128], block_ref[:, 128:])
    shape = (OWNERS, 128)
    index = lax.broadcasted_iota(jnp.int32, shape, 0)
    lane = lax.broadcasted_iota(jnp.int32, shape, 1) & 7
    hits = [jnp.broadcast_to(owners[j : j + 1], shape) == index for j in range(3)]
    named = jnp.zeros(shape, jnp.int32)
    chosen = jnp.zeros(shape, jnp.int32)
    entry = lane * 3
    for j in range(3):
        named = named + jnp.where(hits[j], 1, 0)
        chosen = chosen + jnp.where(hits[j], jnp.broadcast_to(picks[j : j + 1], shape), 0)
        entry = entry + jnp.where(hits[j], j, 0)
    place = group_prefix(named, lane) - named
    for k in range(2):
        mine = (named == 1) & (place == k)
        pick = group_prefix(jnp.where(mine, chosen + 1, 0), lane) - 1
        out[k * OWNERS : (k + 1) * OWNERS, :] = jnp.maximum(pick, 0)
        out[RAW + k * OWNERS : RAW + (k + 1) * OWNERS, :] = pick
        out[ENTRY + k * OWNERS : ENTRY + (k + 1) * OWNERS, :] = group_prefix(
            jnp.where(mine, entry, 0), lane
        )
    for j in range(3):
        owner = owners[j : j + 1]
        at = jnp.minimum(jnp.sum(jnp.where(hits[j], place, 0), axis=0, keepdims=True), 1)
        zo = owner >> 2
        rel = ((owner & 3) - y + NY) & 3
        first = jnp.where(rel == 1, FROM_UP, jnp.where(rel == 2, FROM_FAR, FROM_DOWN))
        out[LISTS + j : LISTS + j + 1, :] = jnp.where(
            rel == 0, zo * RUN + picks[j : j + 1], first + zo * 2 + at
        )


def whole_kernel(
    owner_ref, block_ref, k_ref, v_ref, q_hbm, do_hbm, wq_hbm, wk_hbm, wv_hbm, out,
    tables, idx, tab, stage, ysend, q_ref, do_ref, dq_ref, kl, vl, wacc, gacc, rp,
    halo, glob, wq, wkv, dkv, rsend, ybuf, hbuf, gbuf, acc, zup, zdown,
    total_ref, term, pair, xout, xin,
    ts, ws, zs, zr, ys, yr, hs, hr, gs, gr,
    zs2, zr2, ys2, yr2, hs2, hr2, gs2, gr2, ps, pr, xs, xr
):
    s, z, y = seq_place()
    zu, zd, yp, ym, y2 = neighbours(z, y)
    ypeers = (yp, ym, y2)
    h = lax.axis_index("head")
    x = lax.div(h, 2)
    c = lax.rem(h, 2)
    partner = x * 2 + 1 - c
    xpeers = (lax.rem(x + 1, NX) * 2 + c, lax.rem(x + NX - 1, NX) * 2 + c)
    plane = lax.rem(z, NZ // 2) * (NY * RUN) + RUN - 1
    own = (k_ref, v_ref)

    loads = (
        pltpu.make_async_copy(q_hbm, q_ref, ws.at[0]),
        pltpu.make_async_copy(do_hbm, do_ref, ws.at[1]),
        pltpu.make_async_copy(wq_hbm, wq, ws.at[2]),
        pltpu.make_async_copy(wk_hbm, wkv.at[:, pl.ds(0, HD)], ws.at[3]),
        pltpu.make_async_copy(wv_hbm, wkv.at[:, pl.ds(HD, HD)], ws.at[4]),
    )
    for load in loads:
        load.start()
    greet(
        [("seq", n) for n in (zu, zd, yp, ym, y2)]
        + [("head", n) for n in (partner,) + xpeers]
    )

    def ring(up, t, kv):
        chunk = lax.rem(z + (NZ - t if up else t), NZ)
        where = tab.at[kv, rows_of(chunk * ROWS, ROWS)]
        i = 0 if up else 1
        return send(
            own[kv] if t == 0 else where, where, zs.at[i, t, kv], zr.at[i, t, kv],
            "seq", zu if up else zd,
        )

    def landed(up, t, kv):
        chunk = lax.rem(z + (NZ - 1 - t if up else 1 + t), NZ)
        where = tab.at[kv, rows_of(chunk * ROWS, ROWS)]
        i = 0 if up else 1
        return send(where, where, zs.at[i, t, kv], zr.at[i, t, kv], "seq", zu if up else zd)

    def slot_copy(p, chunk, kv):
        first = (FROM_DOWN, FROM_UP, FROM_FAR)[p]
        at = rows_of((first + chunk * 2) * BLOCK, 2 * BLOCK)
        return send(
            ysend.at[p, chunk, kv], tab.at[kv, at, :], ys.at[p, chunk, kv], yr.at[p, chunk, kv],
            "seq", ypeers[p],
        )

    def global_copy(p, kv):
        return send(
            tab.at[kv, pl.ds(0, 2 * BLOCK), :],
            tab.at[kv, pl.ds((EXTRA + 2) * BLOCK, 2 * BLOCK), :],
            gs.at[p, kv], gr.at[kv], "seq", ypeers[p],
        )

    def halo_copy(p, kv):
        if p == 0:
            row = lax.rem(z + NZ - lax.div(y, 3), NZ) * ROWS + (RUN - 1) * BLOCK
        else:
            row = lax.rem(z + lax.div(3 - y, 3), NZ) * ROWS
        at = pl.ds((EXTRA + p) * BLOCK, BLOCK)
        return send(
            tab.at[kv, rows_of(row, BLOCK), :], tab.at[kv, at, :], hs.at[p, kv], hr.at[p, kv],
            "seq", ypeers[p],
        )

    def spread(chunk, kv):
        stage[kv] = tab[kv, rows_of(chunk * ROWS, ROWS), :].reshape(RUN, BLOCK, HD)
        for p, rel in ((2, 2), (0, 1), (1, 3)):
            for k in range(2):
                pick = idx[k * OWNERS + chunk * NY + y, plane + lax.rem(y + rel, NY) * RUN]
                ysend[p, chunk, kv, k * BLOCK : (k + 1) * BLOCK, :] = stage[kv, pick]
        for p in (2, 0, 1):
            slot_copy(p, chunk, kv).start()

        @pl.when(jnp.logical_and(chunk == 0, y == 0))
        def _():
            for p in range(3):
                global_copy(p, kv).start()

    for kv in range(2):
        ring(True, 0, kv).start()
        ring(False, 0, kv).start()
    index_tables(owner_ref, block_ref, tables, z, y)
    to_scalar = pltpu.make_async_copy(tables, idx, ts)
    to_scalar.start()
    for kv in range(2):
        tab[kv, rows_of(z * ROWS, ROWS), :] = own[kv][...]
    to_scalar.wait()
    for kv in range(2):
        spread(z, kv)
    for t in range(4):
        for kv in range(2):
            ups = (True, False) if t < 3 else ((True,) if kv == 0 else (False,))
            for up in ups:
                landed(up, t, kv).wait_recv()
                if t < 2 or (t == 2 and kv == (0 if up else 1)):
                    ring(up, t + 1, kv).start()
            for up in ups:
                spread(lax.rem(z + (NZ - 1 - t if up else 1 + t), NZ), kv)
            if t == 0:
                for p in range(2):
                    halo_copy(p, kv).start()

    loads[0].wait()
    loads[1].wait()
    wacc[...] = jnp.zeros_like(wacc)
    gacc[...] = jnp.zeros_like(gacc)
    for kv in range(2):
        for p in range(3):
            for n in range(NZ):
                slot_copy(p, n, kv).wait_recv()
        for p in range(2):
            halo_copy(p, kv).wait_recv()

        @pl.when(y == 0)
        def _():
            tab[kv, (EXTRA + 2) * BLOCK : (EXTRA + 4) * BLOCK, :] = tab[kv, 0 : 2 * BLOCK, :]

        @pl.when(y != 0)
        def _():
            global_copy(0, kv).wait_recv()

    def attend(step, carry):
        grads = []
        for n in range(PER):
            b = step * PER + n
            index = [
                jnp.where(b == 0, EXTRA, z * RUN + b - 1),
                z * RUN + b,
                jnp.where(b == RUN - 1, EXTRA + 1, z * RUN + b + 1),
                EXTRA + 2,
                EXTRA + 3,
            ] + [idx[LISTS + j, plane - (RUN - 1) + y * RUN + b] for j in range(3)]
            for j in range(8):
                at = index[j]
                kl[n, j * BLOCK : (j + 1) * BLOCK, :] = tab_blocks[0, at]
                vl[n, j * BLOCK : (j + 1) * BLOCK, :] = tab_blocks[1, at]
        for n in range(PER):
            b = step * PER + n
            mine = rows_of(b * BLOCK, BLOCK)
            q4 = jnp.concatenate([q_ref[mine, g * HD : (g + 1) * HD] for g in range(GROUP)], axis=0)
            d4 = jnp.concatenate([do_ref[mine, g * HD : (g + 1) * HD] for g in range(GROUP)], axis=0)
            keys = kl[n]
            vals = vl[n]
            scores = dot(keys, q4, NT)
            no_left = jnp.logical_and(s == 0, b == 0)
            no_right = jnp.logical_and(s == NZ * NY - 1, b == RUN - 1)
            scores = jnp.concatenate(
                [
                    jnp.where(no_left, -1e30, scores[:BLOCK]),
                    scores[BLOCK : 2 * BLOCK],
                    jnp.where(no_right, -1e30, scores[2 * BLOCK : 3 * BLOCK]),
                    scores[3 * BLOCK :],
                ],
                axis=0,
            )
            row_max = jnp.max(scores, axis=0, keepdims=True)
            powers = jnp.exp((scores - row_max) * SCALE)
            weights = powers * (1.0 / jnp.sum(powers, axis=0, keepdims=True))
            weights_half = weights.astype(jnp.bfloat16)
            dprob = dot(vals, d4, NT)
            delta = jnp.sum(weights_half.astype(jnp.float32) * dprob, axis=0, keepdims=True)
            dscore_half = (weights * (dprob - delta)).astype(jnp.bfloat16)
            dq = (dot(dscore_half, keys, TN) * SCALE).astype(jnp.bfloat16)
            for g in range(GROUP):
                dq_ref[mine, g * HD : (g + 1) * HD] = dq[g * BLOCK : (g + 1) * BLOCK]
            grads.append((dot(dscore_half, q4, NN) * SCALE, dot(weights_half, d4, NN)))
        for n in range(PER):
            b = step * PER + n
            for kv in range(2):
                grad = grads[n][kv]
                wacc[kv, rows_of(b * BLOCK, 3 * BLOCK), :] += grad[: 3 * BLOCK]
                gacc[kv] += grad[3 * BLOCK : 5 * BLOCK]
                for j in range(3):
                    rp[kv, b * 3 + j] = grad[(5 + j) * BLOCK : (6 + j) * BLOCK].astype(jnp.bfloat16)
        return carry

    tab_blocks = tab.reshape(2, TABLE, BLOCK, HD)
    lax.fori_loop(0, RUN // PER, attend, 0)
    for kv in range(2):
        halo[kv, :BLOCK, :] = wacc[kv, :BLOCK, :].astype(jnp.bfloat16)
        halo[kv, BLOCK:, :] = wacc[kv, BLOCK + ROWS :, :].astype(jnp.bfloat16)
        glob[kv] = gacc[kv].astype(jnp.bfloat16)

    def back_copy(p, chunk, kv):
        return send(
            rsend.at[p, chunk, kv], ybuf.at[p, chunk, kv], ys2.at[p, chunk, kv],
            yr2.at[p, chunk, kv], "seq", ypeers[p],
        )

    def halo_back(p):
        half = pl.ds(BLOCK if p == 0 else 0, BLOCK)
        return send(halo.at[:, half, :], hbuf.at[p], hs2.at[p], hr2.at[p], "seq", ypeers[p])

    def global_back(slot):
        return send(glob, gbuf.at[slot], gs2, gr2.at[slot], "seq", z * NY)

    events = [(4, 0, 0), (4, 1, 1)]
    for m in (3, 2, 1):
        events += [(m, 1, 0), (-m, 0, 1), (m, 0, 0), (-m, 1, 1)]
    events += [(0, 0, None), (0, 1, None)]
    low_chunk = lax.rem(z + NZ - lax.div(y, 3), NZ)
    high_chunk = lax.rem(z + lax.div(3 - y, 3), NZ)

    def entry_of(k, chunk, rel):
        return idx[ENTRY + k * OWNERS + chunk * NY + lax.rem(y + rel, NY), plane + y * RUN]

    def offer(event):
        off, kv, _ = event
        chunk = lax.rem(z + off + NZ, NZ)
        for p, rel in ((2, 2), (0, 1), (1, 3)):
            for k in range(2):
                rsend[p, chunk, kv, k * BLOCK : (k + 1) * BLOCK, :] = rp[kv, entry_of(k, chunk, rel)]
        for p in (2, 0, 1):
            back_copy(p, chunk, kv).start()

    def collect(event):
        off, kv, _ = event
        chunk = lax.rem(z + off + NZ, NZ)
        for p in range(3):
            back_copy(p, chunk, kv).wait_recv()
        data = []
        picks = []
        for k in range(2):
            data.append(rp[kv, entry_of(k, chunk, 0)].astype(jnp.float32))
            for p in range(3):
                data.append(
                    ybuf[p, chunk, kv, k * BLOCK : (k + 1) * BLOCK, :].astype(jnp.float32)
                )
            for rel in (0, 3, 1, 2):
                picks.append(
                    idx[RAW + k * OWNERS + chunk * NY + y, plane + lax.rem(y + rel, NY) * RUN]
                )

        def one(b, carry):
            total = jnp.where(picks[0] == b, data[0], 0.0)
            for i in range(1, 8):
                total = total + jnp.where(picks[i] == b, data[i], 0.0)
            acc[kv, rows_of(b * BLOCK, BLOCK), :] = total
            return carry

        lax.fori_loop(0, RUN, one, 0)

        @pl.when(chunk == low_chunk)
        def _():
            acc[kv, (RUN - 1) * BLOCK :, :] += hbuf[1, kv].astype(jnp.float32)

        @pl.when(chunk == high_chunk)
        def _():
            acc[kv, :BLOCK, :] += hbuf[0, kv].astype(jnp.float32)

        @pl.when(jnp.logical_and(chunk == 0, y == 0))
        def _():
            total = glob[kv].astype(jnp.float32)
            for m in range(3):
                total = total + gbuf[m, kv].astype(jnp.float32)
            acc[kv, 0 : 2 * BLOCK, :] += total

    bufs = (zup, zdown)
    zpeer = (zu, zd)

    def zring(i, t, kv):
        return send(
            bufs[i].at[0, t, kv], bufs[i].at[1, t, kv], zs2.at[i, t, kv], zr2.at[i, t, kv],
            "seq", zpeer[i],
        )

    def zpush(event):
        off, kv, i = event
        t = 4 - abs(off)
        total = acc[kv]
        if t >= 2 or (t == 1 and kv == i):
            zring(i, t - 1, kv).wait_recv()
            total = total + bufs[i][1, t - 1, kv].astype(jnp.float32)
        bufs[i][0, t, kv] = total.astype(jnp.bfloat16)
        zring(i, t, kv).start()

    def token_rows(d):
        return rows_of(lax.rem(x + d, NX) * 2 * BLOCK, 2 * BLOCK)

    def query_part(n):
        d = (2, 1, 3, 0)[n // 2]
        a = dq_ref[token_rows(d), :]

        def tile(m, carry):
            w = pl.ds(pl.multiple_of(m * TILE, TILE), TILE)
            total_ref[d, :, w] = dot(a, wq[w, :], NT)
            return carry

        half = D // TILE // 2
        lax.fori_loop(n % 2 * half, n % 2 * half + half, tile, 0)

    halo_back(0).start()
    halo_back(1).start()
    for n in range(1, NY):
        @pl.when(y == n)
        def _():
            global_back(n - 1).start()
    ahead = 6
    for event in events[:ahead]:
        offer(event)
    for load in loads[2:]:
        load.wait()
    query_part(0)
    query_part(1)
    for p in range(2):
        halo_back(p).wait_recv()

    @pl.when(y == 0)
    def _():
        for m in range(3):
            global_back(m).wait_recv()

    parts = 2
    for n, event in enumerate(events[:14]):
        collect(event)
        zpush(event)
        if n + ahead < 16:
            offer(events[n + ahead])
        if n % 2 == 1 and parts < 8:
            query_part(parts)
            parts += 1
    for kv in range(2):
        collect(events[14 + kv])
    for kv in range(2):
        total = acc[kv] + wacc[kv, BLOCK : BLOCK + ROWS, :]
        for i in range(2):
            zring(i, 3, kv).wait_recv()
            total = total + bufs[i][1, 3, kv].astype(jnp.float32)
        dkv[:, kv * HD : (kv + 1) * HD] = total.astype(jnp.bfloat16)

    def cols(quarter):
        return pl.ds(quarter * QUARTER, QUARTER)

    def pair_copy(d, quarter):
        return send(
            term.at[d, rows_of((1 - c) * BLOCK, BLOCK), cols(quarter)],
            pair.at[d, :, cols(quarter)], ps.at[d, quarter], pr.at[d, quarter],
            "head", partner,
        )

    def xring(i, t, quarter):
        return send(
            xout.at[i, t, :, cols(quarter)], xin.at[i, t, :, cols(quarter)],
            xs.at[i, t, quarter], xr.at[i, t, quarter], "head", xpeers[i],
        )

    def compute(d):
        a = dkv[token_rows(d), :]
        for quarter in range(4):
            def tile(n, carry):
                w = pl.ds(pl.multiple_of(quarter * QUARTER + n * TILE, TILE), TILE)
                total = total_ref[d, :, w] + dot(a, wkv[w, :], NT)
                term[d, :, w] = total.astype(jnp.bfloat16)
                return carry

            lax.fori_loop(0, QUARTER // TILE, tile, 0)
            pair_copy(d, quarter).start()

    def both(d, quarter):
        pair_copy(d, quarter).wait_recv()
        mine = term[d, rows_of(c * BLOCK, BLOCK), cols(quarter)].astype(jnp.float32)
        return mine + pair[d, :, cols(quarter)].astype(jnp.float32)

    def arrived(i, t, quarter):
        xring(i, t, quarter).wait_recv()
        return xin[i, t, :, cols(quarter)].astype(jnp.float32)

    def xpush(i, t, quarter, total):
        xout[i, t, :, cols(quarter)] = total.astype(jnp.bfloat16)
        xring(i, t, quarter).start()

    compute(2)
    compute(1)
    for n in range(2):
        xpush(0, 0, n, both(2, n))
        xpush(1, 0, 2 + n, both(2, 2 + n))
    compute(3)
    for n in range(2):
        xpush(0, 1, 2 + n, both(1, 2 + n))
        xpush(1, 1, n, both(3, n))
    compute(0)
    for n in range(2):
        xpush(0, 1, n, both(1, n) + arrived(0, 0, n))
        xpush(1, 1, 2 + n, both(3, 2 + n) + arrived(1, 0, 2 + n))
    for quarter in (2, 3, 0, 1):
        total = both(0, quarter) + arrived(0, 1, quarter) + arrived(1, 1, quarter)
        out[:, cols(quarter)] = total.astype(jnp.bfloat16)

    for i in range(2):
        for t in range(4):
            for kv in range(2):
                if t < 3 or kv == i:
                    ring(i == 0, t, kv).wait_send()
                if t > 0 or kv == i:
                    zring(i, t, kv).wait_send()
    for p in range(3):
        for n in range(NZ):
            for kv in range(2):
                slot_copy(p, n, kv).wait_send()
                back_copy(p, n, kv).wait_send()
    for p in range(2):
        for kv in range(2):
            halo_copy(p, kv).wait_send()
        halo_back(p).wait_send()

    @pl.when(y == 0)
    def _():
        for p in range(3):
            for kv in range(2):
                global_copy(p, kv).wait_send()

    @pl.when(y != 0)
    def _():
        global_back(0).wait_send()

    for d in range(4):
        for quarter in range(4):
            pair_copy(d, quarter).wait_send()
    for i in range(2):
        for quarter in range(4):
            if quarter // 2 == i:
                xring(i, 0, quarter).wait_send()
            xring(i, 1, quarter).wait_send()


def whole(owners, blocks, keys, values, query, grad_out, wq, wk, wv):
    anywhere = pl.BlockSpec(memory_space=pl.ANY)
    half = jnp.bfloat16
    full = jnp.float32
    slots = (3, NZ, 2, 2 * BLOCK, HD)
    return pl.pallas_call(
        whole_kernel,
        out_shape=sds((BLOCK, D)),
        in_specs=[vmem()] * 4 + [anywhere] * 5,
        out_specs=vmem(),
        scratch_shapes=[
            VM((LISTS + 8, 128), jnp.int32),
            pltpu.SMEM((LISTS + 8, 128), jnp.int32),
            VM((2, TABLE * BLOCK, HD), half),
            VM((2, RUN, BLOCK, HD), half),
            VM(slots, half),
            VM((ROWS, GROUP * HD), half),
            VM((ROWS, GROUP * HD), half),
            VM((ROWS, GROUP * HD), half),
            VM((PER, ROWS, HD), half),
            VM((PER, ROWS, HD), half),
            VM((2, ROWS + 2 * BLOCK, HD), full),
            VM((2, 2 * BLOCK, HD), full),
            VM((2, RUN * 3, BLOCK, HD), half),
            VM((2, 2 * BLOCK, HD), half),
            VM((2, 2 * BLOCK, HD), half),
            VM((D, GROUP * HD), half),
            VM((D, 2 * HD), half),
            VM((ROWS, 2 * HD), half),
            VM(slots, half),
            VM(slots, half),
            VM((2, 2, BLOCK, HD), half),
            VM((3, 2, 2 * BLOCK, HD), half),
            VM((2, ROWS, HD), full),
            VM((2, 4, 2, ROWS, HD), half),
            VM((2, 4, 2, ROWS, HD), half),
            VM((4, 2 * BLOCK, D), full),
            VM((4, 2 * BLOCK, D), half),
            VM((4, BLOCK, D), half),
            VM((2, 2, BLOCK, D), half),
            VM((2, 2, BLOCK, D), half),
            DMA,
            DMA((5,)),
            DMA((2, 4, 2)),
            DMA((2, 4, 2)),
            DMA((3, NZ, 2)),
            DMA((3, NZ, 2)),
            DMA((2, 2)),
            DMA((2, 2)),
            DMA((3, 2)),
            DMA((2,)),
            DMA((2, 4, 2)),
            DMA((2, 4, 2)),
            DMA((3, NZ, 2)),
            DMA((3, NZ, 2)),
            DMA((2,)),
            DMA((2,)),
            DMA,
            DMA((3,)),
            DMA((4, 4)),
            DMA((4, 4)),
            DMA((2, 2, 4)),
            DMA((2, 2, 4)),
        ],
        compiler_params=pltpu.CompilerParams(
            collective_id=0, has_side_effects=True, vmem_limit_bytes=60 * 2**20
        ),
        name="whole",
    )(owners, blocks, keys, values, query, grad_out, wq, wk, wv)


def on_device(query, keys, values, grad_out, w_query, w_key, w_value, rand_owner, rand_block):
    return whole(
        rand_owner.T, rand_block.T, keys, values, query, grad_out, w_query, w_key, w_value
    )


def solution(mesh):
    return jax.shard_map(
        on_device,
        mesh=mesh,
        in_specs=(
            P("seq", "head"),
            P("seq", "head"),
            P("seq", "head"),
            P("seq", "head"),
            P(None, "head"),
            P(None, "head"),
            P(None, "head"),
            P(),
            P(),
        ),
        out_specs=P(("seq", "head"), None),
        check_vma=False,
    )
```

time: 400 us -> 105 us (0.26); the launches traced: 395 us -> 105 us
  waiting for transfers between devices: 199 us -> 0 us
  Pallas kernels: 0 us -> 103 us
  local copies, waits for them, and re-layouts: 76.5 us -> 1.87 us
  other arithmetic: 53.7 us -> 0 us
  starting transfers between devices: 29 us -> 0 us
  matrix products: 23.5 us -> 0 us
  between operations: 13.8 us -> 0.01 us
    all_to_all x2 -> x0, waiting for transfers between devices: 157 us -> none  [the longest x1 79.2 us: on_device(): lax.all_to_all(outgoing, 'seq', split_axis=0, concat_axis=0, tiled=True)]
    pallas_call x0 -> x1, Pallas kernels: none -> 103 us  [whole(): pl.pallas_call(whole_kernel, out_shape=sds((BLOCK, D)), in_specs=[vmem()]...]
    reduce_scatter x1 -> x0, waiting for transfers between devices: 36 us -> none  [on_device(): lax.psum_scatter(term.astype(jnp.bfloat16), 'head', scatter_dimension=0,...]
    scatter x2 -> x0, local copies, waits for them, and re-layouts: 34 us -> none  [the longest x1 33.3 us: on_device(): send_index = send_index.at[targets, places_all].set(picks_all, mode='drop')]
    scatter-add x4 -> x0, other arithmetic: 31.5 us -> none  [the longest x1 17 us: on_device(): local_part = local_part.at[send_index].add(arrived.astype(jnp.float32))]
    dot_general x9 -> x0, matrix products: 23.5 us -> none  [the longest x1 6.8 us: on_device(): jnp.einsum('tc,dc->td', grad_values, w_value, preferred_element_type=jnp....]
    all_to_all x2 -> x0, starting transfers between devices: 19 us -> none  [the longest x1 11.7 us: on_device(): lax.all_to_all(outgoing, 'seq', split_axis=0, concat_axis=0, tiled=True)]
    ppermute x4 -> x0, starting transfers between devices: 9.95 us -> none  [the longest x2 7.36 us: with_halo(): before = lax.ppermute(last, axis, up)]
  transfers between devices with their start and end apart: 7 -> 0, of which waited for: 5 -> 0; matrix products, arithmetic and copies ran while one was open for 4% -> 0% of each run, Pallas kernels for 0% -> 0%
where the time goes in v3:
time: 105 us
  Pallas kernels  103 us (98%)
  local copies, waits for them, and re-layouts  1.87 us (2%)
    pallas_call x1, Pallas kernels, whole(): pl.pallas_call(whole_kernel, out_shape=sds((BLOCK, D)), in_specs=[vmem()]...  103 us

profile of v3, /device:TPU:2, one launch (start us, length us, event | category | flops | bytes accessed | tf_op | source)
XLA Modules:
  0.0 104.6 jit_solution(7570517468440668725)
XLA Ops:
  0.0 102.7 %whole.1 = bf16[64,4096]{1,0:T(8,128)(2,1)} custom-call(s32[3,256]{1,0:T(4,128)} %bitcast.2, s32[3,256]{1,0:T(4,128)} %bitcast.3, bf16[512,128]{1,0:T(8,128)(2,1)} %k_ref.1, bf16[512,128]{1,0:T(8,128)(2,1)} %v_ref.1, bf16[512,512]{1,0:T(8,128)(2,1)} %q_hbm.1, bf16[512,512]{1,0:T(8,128)(2,1)} %do_hbm.1, bf16[4096,512]{1,0:T(8,128)(2,1)} %wq_hbm.1, ...), custom_call_target="tpu_custom_call" | custom-call | tf_op jit(solution)/shard_map/whole/pallas_call | solution.py:570
  102.7 1.9 %copy.11 = bf16[64,4096]{1,0:T(8,128)(2,1)} copy(bf16[64,4096]{1,0:T(8,128)(2,1)} %whole.1) | data formatting | bytes 1048576

commit v4 on v3

--- a/solution.py
+++ b/solution.py
@@ -14,6 +14,7 @@
 NX = 4
 RUN = 8
 ROWS = RUN * BLOCK
+HALF = ROWS // 2
 GROUP = 4
 D = 4096
 FROM_UP = NZ * RUN
@@ -128,9 +129,9 @@
 
 
 def whole_kernel(
-    owner_ref, block_ref, k_ref, v_ref, q_hbm, do_hbm, wq_hbm, wk_hbm, wv_hbm, out,
-    tables, idx, tab, stage, ysend, q_ref, do_ref, dq_ref, kl, vl, wacc, gacc, rp,
-    halo, glob, wq, wkv, dkv, rsend, ybuf, hbuf, gbuf, acc, zup, zdown,
+    owner_hbm, block_hbm, k_ref, v_ref, q_hbm, do_hbm, wq_hbm, wk_hbm, wv_hbm, out,
+    owner_ref, block_ref, tables, idx, tab, stage, ysend, q_ref, do_ref, dq_ref, kl, vl, wacc, gacc, rp,
+    halo, glob, wq, wkv, dkv, rsend, ybuf, hbuf, gbuf, pickers, acc, zup, zdown,
     total_ref, term, pair, xout, xin,
     ts, ws, zs, zr, ys, yr, hs, hr, gs, gr,
     zs2, zr2, ys2, yr2, hs2, hr2, gs2, gr2, ps, pr, xs, xr
@@ -153,27 +154,36 @@
         pltpu.make_async_copy(wk_hbm, wkv.at[:, pl.ds(0, HD)], ws.at[3]),
         pltpu.make_async_copy(wv_hbm, wkv.at[:, pl.ds(HD, HD)], ws.at[4]),
     )
-    for load in loads:
+    mine = rows_of(z * ROWS, ROWS)
+    first = (
+        pltpu.make_async_copy(owner_hbm, owner_ref, ws.at[5]),
+        pltpu.make_async_copy(block_hbm, block_ref, ws.at[6]),
+        pltpu.make_async_copy(k_ref, tab.at[0, mine], ws.at[7]),
+        pltpu.make_async_copy(v_ref, tab.at[1, mine], ws.at[8]),
+    )
+    for load in first:
         load.start()
     greet(
         [("seq", n) for n in (zu, zd, yp, ym, y2)]
         + [("head", n) for n in (partner,) + xpeers]
     )
 
-    def ring(up, t, kv):
+    def ring(up, t, kv, half):
         chunk = lax.rem(z + (NZ - t if up else t), NZ)
-        where = tab.at[kv, rows_of(chunk * ROWS, ROWS)]
+        where = tab.at[kv, rows_of(chunk * ROWS + half * HALF, HALF)]
         i = 0 if up else 1
-        return send(
-            own[kv] if t == 0 else where, where, zs.at[i, t, kv], zr.at[i, t, kv],
-            "seq", zu if up else zd,
-        )
-
-    def landed(up, t, kv):
+        n = kv * 2 + half
+        return send(
+            own[kv].at[pl.ds(half * HALF, HALF)] if t == 0 else where, where,
+            zs.at[i, t, n], zr.at[i, t, n], "seq", zu if up else zd,
+        )
+
+    def landed(up, t, kv, half):
         chunk = lax.rem(z + (NZ - 1 - t if up else 1 + t), NZ)
-        where = tab.at[kv, rows_of(chunk * ROWS, ROWS)]
+        where = tab.at[kv, rows_of(chunk * ROWS + half * HALF, HALF)]
         i = 0 if up else 1
-        return send(where, where, zs.at[i, t, kv], zr.at[i, t, kv], "seq", zu if up else zd)
+        n = kv * 2 + half
+        return send(where, where, zs.at[i, t, n], zr.at[i, t, n], "seq", zu if up else zd)
 
     def slot_copy(p, chunk, kv):
         first = (FROM_DOWN, FROM_UP, FROM_FAR)[p]
@@ -216,23 +226,29 @@
                 global_copy(p, kv).start()
 
     for kv in range(2):
-        ring(True, 0, kv).start()
-        ring(False, 0, kv).start()
+        for half in range(2):
+            ring(True, 0, kv, half).start()
+            ring(False, 0, kv, half).start()
+    first[0].wait()
+    first[1].wait()
     index_tables(owner_ref, block_ref, tables, z, y)
     to_scalar = pltpu.make_async_copy(tables, idx, ts)
     to_scalar.start()
-    for kv in range(2):
-        tab[kv, rows_of(z * ROWS, ROWS), :] = own[kv][...]
+    first[2].wait()
+    first[3].wait()
     to_scalar.wait()
     for kv in range(2):
         spread(z, kv)
+    for load in loads:
+        load.start()
     for t in range(4):
         for kv in range(2):
             ups = (True, False) if t < 3 else ((True,) if kv == 0 else (False,))
-            for up in ups:
-                landed(up, t, kv).wait_recv()
-                if t < 2 or (t == 2 and kv == (0 if up else 1)):
-                    ring(up, t + 1, kv).start()
+            for half in range(2):
+                for up in ups:
+                    landed(up, t, kv, half).wait_recv()
+                    if t < 2 or (t == 2 and kv == (0 if up else 1)):
+                        ring(up, t + 1, kv, half).start()
             for up in ups:
                 spread(lax.rem(z + (NZ - 1 - t if up else 1 + t), NZ), kv)
             if t == 0:
@@ -326,12 +342,15 @@
             yr2.at[p, chunk, kv], "seq", ypeers[p],
         )
 
-    def halo_back(p):
+    def halo_back(p, kv):
         half = pl.ds(BLOCK if p == 0 else 0, BLOCK)
-        return send(halo.at[:, half, :], hbuf.at[p], hs2.at[p], hr2.at[p], "seq", ypeers[p])
-
-    def global_back(slot):
-        return send(glob, gbuf.at[slot], gs2, gr2.at[slot], "seq", z * NY)
+        return send(
+            halo.at[kv, half, :], hbuf.at[p, kv], hs2.at[p, kv], hr2.at[p, kv],
+            "seq", ypeers[p],
+        )
+
+    def global_back(slot, kv):
+        return send(glob.at[kv], gbuf.at[slot, kv], gs2.at[kv], gr2.at[slot, kv], "seq", z * NY)
 
     events = [(4, 0, 0), (4, 1, 1)]
     for m in (3, 2, 1):
@@ -352,66 +371,74 @@
         for p in (2, 0, 1):
             back_copy(p, chunk, kv).start()
 
+    done = []
+
     def collect(event):
         off, kv, _ = event
         chunk = lax.rem(z + off + NZ, NZ)
         for p in range(3):
             back_copy(p, chunk, kv).wait_recv()
-        data = []
-        picks = []
-        for k in range(2):
-            data.append(rp[kv, entry_of(k, chunk, 0)].astype(jnp.float32))
-            for p in range(3):
-                data.append(
-                    ybuf[p, chunk, kv, k * BLOCK : (k + 1) * BLOCK, :].astype(jnp.float32)
-                )
-            for rel in (0, 3, 1, 2):
-                picks.append(
+        slot = 1 if off < 0 else 0
+        if (off, 1 - kv) not in done:
+            lane = lax.broadcasted_iota(jnp.int32, (1, HD), 1)
+            row = lax.broadcasted_iota(jnp.int32, (ROWS, HD), 0)
+            for n, rel in enumerate((0, 3, 1, 2)):
+                first, second = [
                     idx[RAW + k * OWNERS + chunk * NY + y, plane + lax.rem(y + rel, NY) * RUN]
-                )
-
-        def one(b, carry):
-            total = jnp.where(picks[0] == b, data[0], 0.0)
-            for i in range(1, 8):
-                total = total + jnp.where(picks[i] == b, data[i], 0.0)
-            acc[kv, rows_of(b * BLOCK, BLOCK), :] = total
-            return carry
-
-        lax.fori_loop(0, RUN, one, 0)
+                    for k in range(2)
+                ]
+                target = jnp.where(lane < BLOCK, first, second) * BLOCK + (lane & (BLOCK - 1))
+                pickers[slot, :, n * HD : (n + 1) * HD] = jnp.where(
+                    row == target, 1.0, 0.0
+                ).astype(jnp.bfloat16)
+        done.append((off, kv))
+        data = [rp[kv, entry_of(k, chunk, 0)] for k in range(2)]
+        data += [ybuf[p, chunk, kv] for p in range(3)]
+        acc[kv] = dot(pickers[slot], jnp.concatenate(data, axis=0), NN)
 
         @pl.when(chunk == low_chunk)
         def _():
+            halo_back(1, kv).wait_recv()
             acc[kv, (RUN - 1) * BLOCK :, :] += hbuf[1, kv].astype(jnp.float32)
 
         @pl.when(chunk == high_chunk)
         def _():
+            halo_back(0, kv).wait_recv()
             acc[kv, :BLOCK, :] += hbuf[0, kv].astype(jnp.float32)
 
         @pl.when(jnp.logical_and(chunk == 0, y == 0))
         def _():
             total = glob[kv].astype(jnp.float32)
             for m in range(3):
+                global_back(m, kv).wait_recv()
                 total = total + gbuf[m, kv].astype(jnp.float32)
             acc[kv, 0 : 2 * BLOCK, :] += total
 
     bufs = (zup, zdown)
     zpeer = (zu, zd)
 
-    def zring(i, t, kv):
-        return send(
-            bufs[i].at[0, t, kv], bufs[i].at[1, t, kv], zs2.at[i, t, kv], zr2.at[i, t, kv],
-            "seq", zpeer[i],
+    def zring(i, t, kv, n):
+        at = pl.ds(n * HALF, HALF) if t < 3 else token_rows(n)
+        return send(
+            bufs[i].at[0, t, kv, at], bufs[i].at[1, t, kv, at], zs2.at[i, t, kv, n],
+            zr2.at[i, t, kv, n], "seq", zpeer[i],
         )
 
     def zpush(event):
         off, kv, i = event
         t = 4 - abs(off)
-        total = acc[kv]
-        if t >= 2 or (t == 1 and kv == i):
-            zring(i, t - 1, kv).wait_recv()
-            total = total + bufs[i][1, t - 1, kv].astype(jnp.float32)
-        bufs[i][0, t, kv] = total.astype(jnp.bfloat16)
-        zring(i, t, kv).start()
+        for half in range(2):
+            at = pl.ds(half * HALF, HALF)
+            total = acc[kv, at, :]
+            if t >= 2 or (t == 1 and kv == i):
+                zring(i, t - 1, kv, half).wait_recv()
+                total = total + bufs[i][1, t - 1, kv, at, :].astype(jnp.float32)
+            bufs[i][0, t, kv, at, :] = total.astype(jnp.bfloat16)
+            if t < 3:
+                zring(i, t, kv, half).start()
+        if t == 3:
+            for d in (2, 1, 3, 0):
+                zring(i, t, kv, d).start()
 
     def token_rows(d):
         return rows_of(lax.rem(x + d, NX) * 2 * BLOCK, 2 * BLOCK)
@@ -428,26 +455,21 @@
         half = D // TILE // 2
         lax.fori_loop(n % 2 * half, n % 2 * half + half, tile, 0)
 
-    halo_back(0).start()
-    halo_back(1).start()
-    for n in range(1, NY):
-        @pl.when(y == n)
-        def _():
-            global_back(n - 1).start()
     ahead = 6
-    for event in events[:ahead]:
+    for n, event in enumerate(events[:ahead]):
+        if n < 2:
+            for m in range(1, NY):
+                @pl.when(y == m)
+                def _():
+                    global_back(m - 1, n).start()
         offer(event)
+    for p in range(2):
+        for kv in range(2):
+            halo_back(p, kv).start()
     for load in loads[2:]:
         load.wait()
     query_part(0)
     query_part(1)
-    for p in range(2):
-        halo_back(p).wait_recv()
-
-    @pl.when(y == 0)
-    def _():
-        for m in range(3):
-            global_back(m).wait_recv()
 
     parts = 2
     for n, event in enumerate(events[:14]):
@@ -460,12 +482,16 @@
             parts += 1
     for kv in range(2):
         collect(events[14 + kv])
-    for kv in range(2):
-        total = acc[kv] + wacc[kv, BLOCK : BLOCK + ROWS, :]
-        for i in range(2):
-            zring(i, 3, kv).wait_recv()
-            total = total + bufs[i][1, 3, kv].astype(jnp.float32)
-        dkv[:, kv * HD : (kv + 1) * HD] = total.astype(jnp.bfloat16)
+
+    def settle(d):
+        at = token_rows(d)
+        shifted = rows_of(lax.rem(x + d, NX) * 2 * BLOCK + BLOCK, 2 * BLOCK)
+        for kv in range(2):
+            total = acc[kv, at, :] + wacc[kv, shifted, :]
+            for i in range(2):
+                zring(i, 3, kv, d).wait_recv()
+                total = total + bufs[i][1, 3, kv, at, :].astype(jnp.float32)
+            dkv[at, kv * HD : (kv + 1) * HD] = total.astype(jnp.bfloat16)
 
     def cols(quarter):
         return pl.ds(quarter * QUARTER, QUARTER)
@@ -484,6 +510,7 @@
         )
 
     def compute(d):
+        settle(d)
         a = dkv[token_rows(d), :]
         for quarter in range(4):
             def tile(n, carry):
@@ -528,10 +555,12 @@
     for i in range(2):
         for t in range(4):
             for kv in range(2):
-                if t < 3 or kv == i:
-                    ring(i == 0, t, kv).wait_send()
-                if t > 0 or kv == i:
-                    zring(i, t, kv).wait_send()
+                for half in range(2):
+                    if t < 3 or kv == i:
+                        ring(i == 0, t, kv, half).wait_send()
+                for n in range(2 if t < 3 else 4):
+                    if t > 0 or kv == i:
+                        zring(i, t, kv, n).wait_send()
     for p in range(3):
         for n in range(NZ):
             for kv in range(2):
@@ -540,7 +569,7 @@
     for p in range(2):
         for kv in range(2):
             halo_copy(p, kv).wait_send()
-        halo_back(p).wait_send()
+            halo_back(p, kv).wait_send()
 
     @pl.when(y == 0)
     def _():
@@ -550,7 +579,8 @@
 
     @pl.when(y != 0)
     def _():
-        global_back(0).wait_send()
+        for kv in range(2):
+            global_back(0, kv).wait_send()
 
     for d in range(4):
         for quarter in range(4):
@@ -563,16 +593,18 @@
 
 
 def whole(owners, blocks, keys, values, query, grad_out, wq, wk, wv):
-    anywhere = pl.BlockSpec(memory_space=pl.ANY)
+    anywhere = pl.BlockSpec(memory_space=pltpu.HBM)
     half = jnp.bfloat16
     full = jnp.float32
     slots = (3, NZ, 2, 2 * BLOCK, HD)
     return pl.pallas_call(
         whole_kernel,
         out_shape=sds((BLOCK, D)),
-        in_specs=[vmem()] * 4 + [anywhere] * 5,
+        in_specs=[anywhere] * 9,
         out_specs=vmem(),
         scratch_shapes=[
+            VM((3, OWNERS * RUN), jnp.int32),
+            VM((3, OWNERS * RUN), jnp.int32),
             VM((LISTS + 8, 128), jnp.int32),
             pltpu.SMEM((LISTS + 8, 128), jnp.int32),
             VM((2, TABLE * BLOCK, HD), half),
@@ -595,6 +627,7 @@
             VM(slots, half),
             VM((2, 2, BLOCK, HD), half),
             VM((3, 2, 2 * BLOCK, HD), half),
+            VM((2, ROWS, ROWS), half),
             VM((2, ROWS, HD), full),
             VM((2, 4, 2, ROWS, HD), half),
             VM((2, 4, 2, ROWS, HD), half),
@@ -604,23 +637,23 @@
             VM((2, 2, BLOCK, D), half),
             VM((2, 2, BLOCK, D), half),
             DMA,
-            DMA((5,)),
-            DMA((2, 4, 2)),
-            DMA((2, 4, 2)),
+            DMA((9,)),
+            DMA((2, 4, 4)),
+            DMA((2, 4, 4)),
             DMA((3, NZ, 2)),
             DMA((3, NZ, 2)),
             DMA((2, 2)),
             DMA((2, 2)),
             DMA((3, 2)),
             DMA((2,)),
-            DMA((2, 4, 2)),
-            DMA((2, 4, 2)),
+            DMA((2, 4, 2, 4)),
+            DMA((2, 4, 2, 4)),
             DMA((3, NZ, 2)),
             DMA((3, NZ, 2)),
+            DMA((2, 2)),
+            DMA((2, 2)),
             DMA((2,)),
-            DMA((2,)),
-            DMA,
-            DMA((3,)),
+            DMA((3, 2)),
             DMA((4, 4)),
             DMA((4, 4)),
             DMA((2, 2, 4)),

time: 105 us -> 104 us (level)
  no operation moved by 1% of the time
where the time goes in v4:
time: 104 us
  Pallas kernels  102 us (98%)
  local copies, waits for them, and re-layouts  1.87 us (2%)
    pallas_call x1, Pallas kernels, whole(): pl.pallas_call(whole_kernel, out_shape=sds((BLOCK, D)), in_specs=[anywher...  102 us

profile of v4, /device:TPU:2, one launch (start us, length us, event | category | flops | bytes accessed | tf_op | source)
XLA Modules:
  0.0 103.6 jit_solution(6169105809037692027)
XLA Ops:
  0.0 101.8 %whole.1 = bf16[64,4096]{1,0:T(8,128)(2,1)} custom-call(s32[3,256]{1,0:T(4,128)} %bitcast.2, s32[3,256]{1,0:T(4,128)} %bitcast.3, bf16[512,128]{1,0:T(8,128)(2,1)} %k_ref.1, bf16[512,128]{1,0:T(8,128)(2,1)} %v_ref.1, bf16[512,512]{1,0:T(8,128)(2,1)} %q_hbm.1, bf16[512,512]{1,0:T(8,128)(2,1)} %do_hbm.1, bf16[4096,512]{1,0:T(8,128)(2,1)} %wq_hbm.1, ...), custom_call_target="tpu_custom_call" | custom-call | tf_op jit(solution)/shard_map/whole/pallas_call | solution.py:600
  101.8 1.9 %copy.11 = bf16[64,4096]{1,0:T(8,128)(2,1)} copy(bf16[64,4096]{1,0:T(8,128)(2,1)} %whole.1) | data formatting | bytes 1048576

commit v5 on v4

--- a/solution.py
+++ b/solution.py
@@ -21,11 +21,16 @@
 FROM_DOWN = FROM_UP + 2 * NZ
 FROM_FAR = FROM_DOWN + 2 * NZ
 EXTRA = FROM_FAR + 2 * NZ
-TABLE = EXTRA + 4
+OPPOSITE = EXTRA + 4
+TABLE = OPPOSITE + 2
 OWNERS = NZ * NY
 RAW = 2 * OWNERS
 ENTRY = 4 * OWNERS
 LISTS = 6 * OWNERS
+FAR = LISTS + 8
+FAR_RAW = FAR + 2 * OWNERS
+INDEX_ROWS = FAR_RAW + 2 * OWNERS
+NEAR = (0, 1, 2, 3, 5, 6, 7)
 QUARTER = D // 4
 TILE = 512
 PER = 2
@@ -93,13 +98,8 @@
     return value
 
 
-def index_tables(owner_ref, block_ref, out, z, y):
-    low = z < NZ // 2
-    owners = jnp.where(low, owner_ref[:, :128], owner_ref[:, 128:])
-    picks = jnp.where(low, block_ref[:, :128], block_ref[:, 128:])
-    shape = (OWNERS, 128)
-    index = lax.broadcasted_iota(jnp.int32, shape, 0)
-    lane = lax.broadcasted_iota(jnp.int32, shape, 1) & 7
+def place_table(owners, picks, index, lane):
+    shape = index.shape
     hits = [jnp.broadcast_to(owners[j : j + 1], shape) == index for j in range(3)]
     named = jnp.zeros(shape, jnp.int32)
     chosen = jnp.zeros(shape, jnp.int32)
@@ -109,13 +109,24 @@
         chosen = chosen + jnp.where(hits[j], jnp.broadcast_to(picks[j : j + 1], shape), 0)
         entry = entry + jnp.where(hits[j], j, 0)
     place = group_prefix(named, lane) - named
+    mine = [(named == 1) & (place == k) for k in range(2)]
+    table = [group_prefix(jnp.where(m, chosen + 1, 0), lane) - 1 for m in mine]
+    return hits, entry, place, mine, table
+
+
+def index_tables(owner_ref, block_ref, out, z, y):
+    low = z < NZ // 2
+    owners = jnp.where(low, owner_ref[:, :128], owner_ref[:, 128:])
+    picks = jnp.where(low, block_ref[:, :128], block_ref[:, 128:])
+    shape = (OWNERS, 128)
+    index = lax.broadcasted_iota(jnp.int32, shape, 0)
+    lane = lax.broadcasted_iota(jnp.int32, shape, 1) & 7
+    hits, entry, place, mine, table = place_table(owners, picks, index, lane)
     for k in range(2):
-        mine = (named == 1) & (place == k)
-        pick = group_prefix(jnp.where(mine, chosen + 1, 0), lane) - 1
-        out[k * OWNERS : (k + 1) * OWNERS, :] = jnp.maximum(pick, 0)
-        out[RAW + k * OWNERS : RAW + (k + 1) * OWNERS, :] = pick
+        out[k * OWNERS : (k + 1) * OWNERS, :] = jnp.maximum(table[k], 0)
+        out[RAW + k * OWNERS : RAW + (k + 1) * OWNERS, :] = table[k]
         out[ENTRY + k * OWNERS : ENTRY + (k + 1) * OWNERS, :] = group_prefix(
-            jnp.where(mine, entry, 0), lane
+            jnp.where(mine[k], entry, 0), lane
         )
     for j in range(3):
         owner = owners[j : j + 1]
@@ -123,18 +134,26 @@
         zo = owner >> 2
         rel = ((owner & 3) - y + NY) & 3
         first = jnp.where(rel == 1, FROM_UP, jnp.where(rel == 2, FROM_FAR, FROM_DOWN))
-        out[LISTS + j : LISTS + j + 1, :] = jnp.where(
-            rel == 0, zo * RUN + picks[j : j + 1], first + zo * 2 + at
-        )
+        column = jnp.where(
+            zo == lax.rem(z + NZ // 2, NZ), OPPOSITE + at, zo * RUN + picks[j : j + 1]
+        )
+        out[LISTS + j : LISTS + j + 1, :] = jnp.where(rel == 0, column, first + zo * 2 + at)
+    owners = jnp.where(low, owner_ref[:, 128:], owner_ref[:, :128])
+    picks = jnp.where(low, block_ref[:, 128:], block_ref[:, :128])
+    table = place_table(owners, picks, index, lane)[4]
+    for k in range(2):
+        out[FAR + k * OWNERS : FAR + (k + 1) * OWNERS, :] = jnp.maximum(table[k], 0)
+        out[FAR_RAW + k * OWNERS : FAR_RAW + (k + 1) * OWNERS, :] = table[k]
 
 
 def whole_kernel(
     owner_hbm, block_hbm, k_ref, v_ref, q_hbm, do_hbm, wq_hbm, wk_hbm, wv_hbm, out,
-    owner_ref, block_ref, tables, idx, tab, stage, ysend, q_ref, do_ref, dq_ref, kl, vl, wacc, gacc, rp,
-    halo, glob, wq, wkv, dkv, rsend, ybuf, hbuf, gbuf, pickers, acc, zup, zdown,
+    owner_ref, block_ref, tables, idx, tab, stage, ysend, osend, q_ref, do_ref, dq_ref, kl, vl, wacc, gacc, rp,
+    halo, glob, wq, wkv, dkv, rsend, ybuf, obuf, hbuf, gbuf, pickers, acc, zup, zdown,
     total_ref, term, pair, xout, xin,
     ts, ws, zs, zr, ys, yr, hs, hr, gs, gr,
-    zs2, zr2, ys2, yr2, hs2, hr2, gs2, gr2, ps, pr, xs, xr
+    zs2, zr2, ys2, yr2, hs2, hr2, gs2, gr2, ps, pr, xs, xr,
+    os1, or1, os2, or2, og
 ):
     s, z, y = seq_place()
     zu, zd, yp, ym, y2 = neighbours(z, y)
@@ -146,6 +165,8 @@
     xpeers = (lax.rem(x + 1, NX) * 2 + c, lax.rem(x + NX - 1, NX) * 2 + c)
     plane = lax.rem(z, NZ // 2) * (NY * RUN) + RUN - 1
     own = (k_ref, v_ref)
+    opp = lax.rem(z + NZ // 2, NZ)
+    near = [lax.rem(z + n, NZ) for n in NEAR]
 
     loads = (
         pltpu.make_async_copy(q_hbm, q_ref, ws.at[0]),
@@ -165,6 +186,7 @@
         load.start()
     greet(
         [("seq", n) for n in (zu, zd, yp, ym, y2)]
+        + [("seq", opp * NY + n) for n in range(NY)]
         + [("head", n) for n in (partner,) + xpeers]
     )
 
@@ -191,6 +213,21 @@
         return send(
             ysend.at[p, chunk, kv], tab.at[kv, at, :], ys.at[p, chunk, kv], yr.at[p, chunk, kv],
             "seq", ypeers[p],
+        )
+
+    def opposite_copy(rel, chunk, kv):
+        first = (OPPOSITE, FROM_DOWN + chunk * 2, FROM_FAR + chunk * 2, FROM_UP + chunk * 2)[rel]
+        at = rows_of(first * BLOCK, 2 * BLOCK)
+        return send(
+            osend.at[rel, kv], tab.at[kv, at, :], os1.at[rel, kv], or1.at[rel, kv],
+            "seq", opp * NY + lax.rem(y + rel, NY),
+        )
+
+    def opposite_global(n, kv):
+        return send(
+            tab.at[kv, pl.ds(0, 2 * BLOCK), :],
+            tab.at[kv, pl.ds((EXTRA + 2) * BLOCK, 2 * BLOCK), :],
+            og.at[n, kv], gr.at[kv], "seq", opp * NY + n,
         )
 
     def global_copy(p, kv):
@@ -239,21 +276,32 @@
     to_scalar.wait()
     for kv in range(2):
         spread(z, kv)
+        for rel in range(NY):
+            for k in range(2):
+                pick = idx[FAR + k * OWNERS + z * NY + y, plane + lax.rem(y + rel, NY) * RUN]
+                osend[rel, kv, k * BLOCK : (k + 1) * BLOCK, :] = stage[kv, pick]
     for load in loads:
         load.start()
-    for t in range(4):
+    for t in range(3):
         for kv in range(2):
-            ups = (True, False) if t < 3 else ((True,) if kv == 0 else (False,))
             for half in range(2):
-                for up in ups:
+                for up in (True, False):
                     landed(up, t, kv, half).wait_recv()
-                    if t < 2 or (t == 2 and kv == (0 if up else 1)):
+                    if t < 2:
                         ring(up, t + 1, kv, half).start()
-            for up in ups:
+            for up in (True, False):
                 spread(lax.rem(z + (NZ - 1 - t if up else 1 + t), NZ), kv)
             if t == 0:
                 for p in range(2):
                     halo_copy(p, kv).start()
+            if t == 1:
+                for rel in (2, 1, 3, 0):
+                    opposite_copy(rel, z, kv).start()
+
+                @pl.when(s == 0)
+                def _():
+                    for n in range(NY):
+                        opposite_global(n, kv).start()
 
     loads[0].wait()
     loads[1].wait()
@@ -261,16 +309,18 @@
     gacc[...] = jnp.zeros_like(gacc)
     for kv in range(2):
         for p in range(3):
-            for n in range(NZ):
-                slot_copy(p, n, kv).wait_recv()
+            for chunk in near:
+                slot_copy(p, chunk, kv).wait_recv()
         for p in range(2):
             halo_copy(p, kv).wait_recv()
-
-        @pl.when(y == 0)
+        for rel in range(NY):
+            opposite_copy(rel, opp, kv).wait_recv()
+
+        @pl.when(jnp.logical_and(y == 0, z != NZ // 2))
         def _():
             tab[kv, (EXTRA + 2) * BLOCK : (EXTRA + 4) * BLOCK, :] = tab[kv, 0 : 2 * BLOCK, :]
 
-        @pl.when(y != 0)
+        @pl.when(jnp.logical_or(y != 0, z == NZ // 2))
         def _():
             global_copy(0, kv).wait_recv()
 
@@ -350,9 +400,35 @@
         )
 
     def global_back(slot, kv):
-        return send(glob.at[kv], gbuf.at[slot, kv], gs2.at[kv], gr2.at[slot, kv], "seq", z * NY)
-
-    events = [(4, 0, 0), (4, 1, 1)]
+        return send(
+            glob.at[kv], gbuf.at[slot, kv], gs2.at[kv], gr2.at[slot, kv], "seq",
+            z * NY if slot < 3 else 0,
+        )
+
+    def opposite_back(rel, kv):
+        return send(
+            osend.at[rel, kv], obuf.at[rel, kv], os2.at[rel, kv], or2.at[rel, kv],
+            "seq", opp * NY + lax.rem(y + rel, NY),
+        )
+
+    def offer_opposite(kv):
+        for rel in range(NY):
+            opposite_copy(rel, z, kv).wait_send()
+        for rel in range(NY):
+            for k in range(2):
+                osend[rel, kv, k * BLOCK : (k + 1) * BLOCK, :] = rp[kv, entry_of(k, opp, rel)]
+        for rel in (2, 1, 3, 0):
+            opposite_back(rel, kv).start()
+
+    def select(slot, n, first, second):
+        lane = lax.broadcasted_iota(jnp.int32, (1, HD), 1)
+        row = lax.broadcasted_iota(jnp.int32, (ROWS, HD), 0)
+        target = jnp.where(lane < BLOCK, first, second) * BLOCK + (lane & (BLOCK - 1))
+        pickers[slot, :, n * HD : (n + 1) * HD] = jnp.where(
+            row == target, 1.0, 0.0
+        ).astype(jnp.bfloat16)
+
+    events = []
     for m in (3, 2, 1):
         events += [(m, 1, 0), (-m, 0, 1), (m, 0, 0), (-m, 1, 1)]
     events += [(0, 0, None), (0, 1, None)]
@@ -380,21 +456,29 @@
             back_copy(p, chunk, kv).wait_recv()
         slot = 1 if off < 0 else 0
         if (off, 1 - kv) not in done:
-            lane = lax.broadcasted_iota(jnp.int32, (1, HD), 1)
-            row = lax.broadcasted_iota(jnp.int32, (ROWS, HD), 0)
             for n, rel in enumerate((0, 3, 1, 2)):
                 first, second = [
                     idx[RAW + k * OWNERS + chunk * NY + y, plane + lax.rem(y + rel, NY) * RUN]
                     for k in range(2)
                 ]
-                target = jnp.where(lane < BLOCK, first, second) * BLOCK + (lane & (BLOCK - 1))
-                pickers[slot, :, n * HD : (n + 1) * HD] = jnp.where(
-                    row == target, 1.0, 0.0
-                ).astype(jnp.bfloat16)
+                select(slot, n, first, second)
+            if off == 0:
+                for rel in range(NY):
+                    lane = plane + lax.rem(y + NY - rel, NY) * RUN
+                    first, second = [
+                        idx[FAR_RAW + k * OWNERS + z * NY + y, lane] for k in range(2)
+                    ]
+                    select(2, rel, first, second)
         done.append((off, kv))
         data = [rp[kv, entry_of(k, chunk, 0)] for k in range(2)]
         data += [ybuf[p, chunk, kv] for p in range(3)]
-        acc[kv] = dot(pickers[slot], jnp.concatenate(data, axis=0), NN)
+        sums = dot(pickers[slot], jnp.concatenate(data, axis=0), NN)
+        if off == 0:
+            for rel in range(NY):
+                opposite_back(rel, kv).wait_recv()
+            data = [obuf[rel, kv] for rel in range(NY)]
+            sums = sums + dot(pickers[2], jnp.concatenate(data, axis=0), NN)
+        acc[kv] = sums
 
         @pl.when(chunk == low_chunk)
         def _():
@@ -414,11 +498,20 @@
                 total = total + gbuf[m, kv].astype(jnp.float32)
             acc[kv, 0 : 2 * BLOCK, :] += total
 
+        if off == 0:
+            @pl.when(s == 0)
+            def _():
+                total = jnp.zeros((2 * BLOCK, HD), jnp.float32)
+                for m in range(3, 7):
+                    global_back(m, kv).wait_recv()
+                    total = total + gbuf[m, kv].astype(jnp.float32)
+                acc[kv, 0 : 2 * BLOCK, :] += total
+
     bufs = (zup, zdown)
     zpeer = (zu, zd)
 
     def zring(i, t, kv, n):
-        at = pl.ds(n * HALF, HALF) if t < 3 else token_rows(n)
+        at = pl.ds(n * HALF, HALF) if t < 2 else token_rows(n)
         return send(
             bufs[i].at[0, t, kv, at], bufs[i].at[1, t, kv, at], zs2.at[i, t, kv, n],
             zr2.at[i, t, kv, n], "seq", zpeer[i],
@@ -426,17 +519,17 @@
 
     def zpush(event):
         off, kv, i = event
-        t = 4 - abs(off)
+        t = 3 - abs(off)
         for half in range(2):
             at = pl.ds(half * HALF, HALF)
             total = acc[kv, at, :]
-            if t >= 2 or (t == 1 and kv == i):
+            if t >= 1:
                 zring(i, t - 1, kv, half).wait_recv()
                 total = total + bufs[i][1, t - 1, kv, at, :].astype(jnp.float32)
             bufs[i][0, t, kv, at, :] = total.astype(jnp.bfloat16)
-            if t < 3:
+            if t < 2:
                 zring(i, t, kv, half).start()
-        if t == 3:
+        if t == 2:
             for d in (2, 1, 3, 0):
                 zring(i, t, kv, d).start()
 
@@ -458,10 +551,15 @@
     ahead = 6
     for n, event in enumerate(events[:ahead]):
         if n < 2:
-            for m in range(1, NY):
-                @pl.when(y == m)
+            for m in range(NY):
+                if m > 0:
+                    @pl.when(jnp.logical_and(y == m, z != NZ // 2))
+                    def _():
+                        global_back(m - 1, n).start()
+
+                @pl.when(jnp.logical_and(y == m, z == NZ // 2))
                 def _():
-                    global_back(m - 1, n).start()
+                    global_back(3 + m, n).start()
         offer(event)
     for p in range(2):
         for kv in range(2):
@@ -472,16 +570,18 @@
     query_part(1)
 
     parts = 2
-    for n, event in enumerate(events[:14]):
+    for n, event in enumerate(events[:12]):
         collect(event)
         zpush(event)
-        if n + ahead < 16:
+        if n + ahead < 14:
             offer(events[n + ahead])
+        if n in (5, 6):
+            offer_opposite(n - 5)
         if n % 2 == 1 and parts < 8:
             query_part(parts)
             parts += 1
     for kv in range(2):
-        collect(events[14 + kv])
+        collect(events[12 + kv])
 
     def settle(d):
         at = token_rows(d)
@@ -489,8 +589,8 @@
         for kv in range(2):
             total = acc[kv, at, :] + wacc[kv, shifted, :]
             for i in range(2):
-                zring(i, 3, kv, d).wait_recv()
-                total = total + bufs[i][1, 3, kv, at, :].astype(jnp.float32)
+                zring(i, 2, kv, d).wait_recv()
+                total = total + bufs[i][1, 2, kv, at, :].astype(jnp.float32)
             dkv[at, kv * HD : (kv + 1) * HD] = total.astype(jnp.bfloat16)
 
     def cols(quarter):
@@ -553,31 +653,39 @@
         out[:, cols(quarter)] = total.astype(jnp.bfloat16)
 
     for i in range(2):
-        for t in range(4):
+        for t in range(3):
             for kv in range(2):
                 for half in range(2):
-                    if t < 3 or kv == i:
-                        ring(i == 0, t, kv, half).wait_send()
-                for n in range(2 if t < 3 else 4):
-                    if t > 0 or kv == i:
-                        zring(i, t, kv, n).wait_send()
+                    ring(i == 0, t, kv, half).wait_send()
+                for n in range(2 if t < 2 else 4):
+                    zring(i, t, kv, n).wait_send()
     for p in range(3):
-        for n in range(NZ):
+        for chunk in near:
             for kv in range(2):
-                slot_copy(p, n, kv).wait_send()
-                back_copy(p, n, kv).wait_send()
+                slot_copy(p, chunk, kv).wait_send()
+                back_copy(p, chunk, kv).wait_send()
+    for rel in range(NY):
+        for kv in range(2):
+            opposite_back(rel, kv).wait_send()
+
+    @pl.when(s == 0)
+    def _():
+        for n in range(NY):
+            for kv in range(2):
+                opposite_global(n, kv).wait_send()
+
     for p in range(2):
         for kv in range(2):
             halo_copy(p, kv).wait_send()
             halo_back(p, kv).wait_send()
 
-    @pl.when(y == 0)
+    @pl.when(jnp.logical_and(y == 0, z != NZ // 2))
     def _():
         for p in range(3):
             for kv in range(2):
                 global_copy(p, kv).wait_send()
 
-    @pl.when(y != 0)
+    @pl.when(jnp.logical_or(y != 0, z == NZ // 2))
     def _():
         for kv in range(2):
             global_back(0, kv).wait_send()
@@ -605,11 +713,12 @@
         scratch_shapes=[
             VM((3, OWNERS * RUN), jnp.int32),
             VM((3, OWNERS * RUN), jnp.int32),
-            VM((LISTS + 8, 128), jnp.int32),
-            pltpu.SMEM((LISTS + 8, 128), jnp.int32),
+            VM((INDEX_ROWS, 128), jnp.int32),
+            pltpu.SMEM((INDEX_ROWS, 128), jnp.int32),
             VM((2, TABLE * BLOCK, HD), half),
             VM((2, RUN, BLOCK, HD), half),
             VM(slots, half),
+            VM((NY, 2, 2 * BLOCK, HD), half),
             VM((ROWS, GROUP * HD), half),
             VM((ROWS, GROUP * HD), half),
             VM((ROWS, GROUP * HD), half),
@@ -625,9 +734,10 @@
             VM((ROWS, 2 * HD), half),
             VM(slots, half),
             VM(slots, half),
+            VM((NY, 2, 2 * BLOCK, HD), half),
             VM((2, 2, BLOCK, HD), half),
-            VM((3, 2, 2 * BLOCK, HD), half),
-            VM((2, ROWS, ROWS), half),
+            VM((7, 2, 2 * BLOCK, HD), half),
+            VM((3, ROWS, ROWS), half),
             VM((2, ROWS, HD), full),
             VM((2, 4, 2, ROWS, HD), half),
             VM((2, 4, 2, ROWS, HD), half),
@@ -653,11 +763,16 @@
             DMA((2, 2)),
             DMA((2, 2)),
             DMA((2,)),
-            DMA((3, 2)),
+            DMA((7, 2)),
             DMA((4, 4)),
             DMA((4, 4)),
             DMA((2, 2, 4)),
             DMA((2, 2, 4)),
+            DMA((NY, 2)),
+            DMA((NY, 2)),
+            DMA((NY, 2)),
+            DMA((NY, 2)),
+            DMA((NY, 2)),
         ],
         compiler_params=pltpu.CompilerParams(
             collective_id=0, has_side_effects=True, vmem_limit_bytes=60 * 2**20

time: 104 us -> 120 us (1.15)
  Pallas kernels: 102 us -> 117 us
    pallas_call x1, Pallas kernels: 102 us -> 117 us  [whole(): pl.pallas_call(whole_kernel, out_shape=sds((BLOCK, D)), in_specs=[anywher...]
where the time goes in v5:
time: 120 us; the launch traced here: 119 us
  Pallas kernels  117 us (98%)
  local copies, waits for them, and re-layouts  1.87 us (2%)
    pallas_call x1, Pallas kernels, whole(): pl.pallas_call(whole_kernel, out_shape=sds((BLOCK, D)), in_specs=[anywher...  117 us

profile of v5, /device:TPU:2, one launch (start us, length us, event | category | flops | bytes accessed | tf_op | source)
XLA Modules:
  0.0 118.7 jit_solution(9837769833610064223)
XLA Ops:
  0.0 116.8 %whole.1 = bf16[64,4096]{1,0:T(8,128)(2,1)} custom-call(s32[3,256]{1,0:T(4,128)} %bitcast.2, s32[3,256]{1,0:T(4,128)} %bitcast.3, bf16[512,128]{1,0:T(8,128)(2,1)} %k_ref.1, bf16[512,128]{1,0:T(8,128)(2,1)} %v_ref.1, bf16[512,512]{1,0:T(8,128)(2,1)} %q_hbm.1, bf16[512,512]{1,0:T(8,128)(2,1)} %do_hbm.1, bf16[4096,512]{1,0:T(8,128)(2,1)} %wq_hbm.1, ...), custom_call_target="tpu_custom_call" | custom-call | tf_op jit(solution)/shard_map/whole/pallas_call | solution.py:708
  116.8 1.9 %copy.11 = bf16[64,4096]{1,0:T(8,128)(2,1)} copy(bf16[64,4096]{1,0:T(8,128)(2,1)} %whole.1) | data formatting | bytes 1048576

commit v6 on v4

--- a/solution.py
+++ b/solution.py
@@ -217,7 +217,7 @@
             for k in range(2):
                 pick = idx[k * OWNERS + chunk * NY + y, plane + lax.rem(y + rel, NY) * RUN]
                 ysend[p, chunk, kv, k * BLOCK : (k + 1) * BLOCK, :] = stage[kv, pick]
-        for p in (2, 0, 1):
+        for p in (0, 1, 2):
             slot_copy(p, chunk, kv).start()
 
         @pl.when(jnp.logical_and(chunk == 0, y == 0))
@@ -315,7 +315,7 @@
             dprob = dot(vals, d4, NT)
             delta = jnp.sum(weights_half.astype(jnp.float32) * dprob, axis=0, keepdims=True)
             dscore_half = (weights * (dprob - delta)).astype(jnp.bfloat16)
-            dq = (dot(dscore_half, keys, TN) * SCALE).astype(jnp.bfloat16)
+            dq = (dot(keys, dscore_half, TN) * SCALE).T.astype(jnp.bfloat16)
             for g in range(GROUP):
                 dq_ref[mine, g * HD : (g + 1) * HD] = dq[g * BLOCK : (g + 1) * BLOCK]
             grads.append((dot(dscore_half, q4, NN) * SCALE, dot(weights_half, d4, NN)))
@@ -368,7 +368,7 @@
         for p, rel in ((2, 2), (0, 1), (1, 3)):
             for k in range(2):
                 rsend[p, chunk, kv, k * BLOCK : (k + 1) * BLOCK, :] = rp[kv, entry_of(k, chunk, rel)]
-        for p in (2, 0, 1):
+        for p in (0, 1, 2):
             back_copy(p, chunk, kv).start()
 
     done = []
@@ -455,7 +455,7 @@
         half = D // TILE // 2
         lax.fori_loop(n % 2 * half, n % 2 * half + half, tile, 0)
 
-    ahead = 6
+    ahead = 5
     for n, event in enumerate(events[:ahead]):
         if n < 2:
             for m in range(1, NY):

time: 104 us -> 103 us (level)
  no operation moved by 1% of the time
where the time goes in v6:
time: 103 us
  Pallas kernels  101 us (98%)
  local copies, waits for them, and re-layouts  1.87 us (2%)
    pallas_call x1, Pallas kernels, whole(): pl.pallas_call(whole_kernel, out_shape=sds((BLOCK, D)), in_specs=[anywher...  101 us

profile of v6, /device:TPU:2, one launch (start us, length us, event | category | flops | bytes accessed | tf_op | source)
XLA Modules:
  0.0 102.7 jit_solution(12802301459711499461)
XLA Ops:
  0.0 100.8 %whole.1 = bf16[64,4096]{1,0:T(8,128)(2,1)} custom-call(s32[3,256]{1,0:T(4,128)} %bitcast.2, s32[3,256]{1,0:T(4,128)} %bitcast.3, bf16[512,128]{1,0:T(8,128)(2,1)} %k_ref.1, bf16[512,128]{1,0:T(8,128)(2,1)} %v_ref.1, bf16[512,512]{1,0:T(8,128)(2,1)} %q_hbm.1, bf16[512,512]{1,0:T(8,128)(2,1)} %do_hbm.1, bf16[4096,512]{1,0:T(8,128)(2,1)} %wq_hbm.1, ...), custom_call_target="tpu_custom_call" | custom-call | tf_op jit(solution)/shard_map/whole/pallas_call | solution.py:600
  100.8 1.9 %copy.11 = bf16[64,4096]{1,0:T(8,128)(2,1)} copy(bf16[64,4096]{1,0:T(8,128)(2,1)} %whole.1) | data formatting | bytes 1048576
